TPU v7x, 128 devices: a whole 4x4x4 slice. The times are simulated.
128 devices in a mesh: gx: 2 (over core), gy: 64 (over z, y, x).
Axes of the slice: x: 4, y: 4, z: 4, core: 2. Of those that a mesh axis runs over, the one named last changes fastest.
Arguments:
- velocity: float32 [2, 32, 256, 8192], P(None, None, 'gx', 'gy'), may hold values from -2.5 to 2.5
- stream_metric: float32 [256], replicated, may hold values from 0.5 to 2
- wall_metric: float32 [8192], replicated, may hold values from 0.5 to 2
Outputs:
- advection: float32 [3, 32, 256, 8192], P(None, None, 'gx', 'gy')
All inputs are finite; a program needn't handle non-finite values.
Results may differ from a plain program's by a relative error of at most 0.0003.
Values sent between devices are 32-bit elements; how exact they have to be, the bound alone decides.
A program may use at most 256 MiB of HBM per device.

v0:
```python
import functools

import jax
import jax.numpy as jnp
from jax import lax
from jax.experimental import pallas as pl
from jax.experimental.pallas import tpu as pltpu
from jax.sharding import PartitionSpec as P

MESH = pl.DeviceIdType.MESH
F32 = jnp.float32
L = 128
HALO = 8
EDGE = 4
WIDE = L + 2 * HALO
SPAN = L + 2 * EDGE
CENTRAL = (45.0, -9.0, 1.0)
INTERIOR = (-1.0 / 60.0, 0.15, -0.75, 0.0, 0.75, -0.15, 1.0 / 60.0)
ROW_FIRST = (0.0, 0.0, 0.0, -11.0 / 6.0, 3.0, -1.5, 1.0 / 3.0)
ROW_SECOND = (0.0, 0.0, -1.0 / 3.0, -0.5, 1.0, -1.0 / 6.0, 0.0)
ROW_THIRD = (0.0, 1.0 / 12.0, -2.0 / 3.0, 0.0, 2.0 / 3.0, -1.0 / 12.0, 0.0)
ROW_SECOND_LAST = (0.0, 1.0 / 6.0, -1.0, 0.5, 1.0 / 3.0, 0.0, 0.0)
ROW_LAST = (-1.0 / 3.0, 1.5, -3.0, 11.0 / 6.0, 0.0, 0.0, 0.0)
TILES = SPAN // 8
GROUPS = -(-TILES // 4)
ROW_FRAC, ROW_SLOTS, ROW_EDGES = 7, 8, 12
ROWS = 18
FRONT, BACK, NEXT, PREV = range(4)


def rings_of(count):
    size = 4 if count % 4 == 0 and count > 16 else 2
    rings, stride = [], 1
    while stride < count:
        rings.append((stride, size))
        stride *= size
    return rings


def lanes(shape):
    return lax.broadcasted_iota(jnp.int32, shape, len(shape) - 1)


def rolled(x, shift):
    if isinstance(shift, int):
        shift %= L
        if shift == 0:
            return x
    return pltpu.roll(x, shift, len(x.shape) - 1)


def running(x):
    lane = lanes(x.shape)
    step = 1
    while step < L:
        x = x + jnp.where(lane >= step, rolled(x, step), 0.0)
        step *= 2
    return x


def scaled(x, weight):
    return x if weight == 1.0 else x * weight


def chunks(total, size):
    return [(i, min(size, total - i)) for i in range(0, total, size)]


def skew(adv, fields):
    centre = adv(0)
    sums = [None] * len(fields)
    for d, weight in enumerate(CENTRAL, start=1):
        up = scaled(centre + adv(d), weight)
        down = scaled(centre + adv(-d), weight)
        for n, field in enumerate(fields):
            term = up * field(d) - down * field(-d)
            sums[n] = term if sums[n] is None else sums[n] + term
    return sums


def slope_sum(field):
    total = None
    for d, weight in enumerate(CENTRAL, start=1):
        term = scaled(field(d) - field(-d), weight)
        total = term if total is None else total + term
    return total


def first_kernel(
    n_gy, depth,
    vel, sm, wm,
    uw, crow, halo, chalo, part, below_total, rows, m120,
    slope, m_wide, pack, spack, sland, stage_out, stage_in, tot_pack,
    load_sem, gx_send, gx_recv, y_send, y_recv, st_send, st_recv,
):
    gx, gy = lax.axis_index("gx"), lax.axis_index("gy")
    other = 1 - gx
    rings = rings_of(n_gy)
    up_gy, down_gy = lax.rem(gy + 1, n_gy), lax.rem(gy + n_gy - 1, n_gy)

    def peer(stride, size, offset):
        place = lax.rem(gy // stride, size)
        return gy + (lax.rem(place + offset, size) - place) * stride

    half = depth // 2
    loads = []
    for f in range(2):
        for h in range(2):
            loads.append(pltpu.make_async_copy(
                vel.at[f, pl.ds(h * half, half)],
                uw.at[f, pl.ds(h * half, half), pl.ds(HALO, L)],
                load_sem.at[f, h]))
            loads[-1].start()

    barrier = pltpu.get_barrier_semaphore()
    count = 0
    targets = [{"gx": other}, {"gy": up_gy}, {"gy": down_gy}]
    for stride, size in rings:
        targets += [{"gy": peer(stride, size, o)} for o in range(1, size)]
    for target in targets:
        pl.semaphore_signal(barrier, inc=1, device_id=target, device_id_type=MESH)
        count += 1

    rid = lax.broadcasted_iota(jnp.int32, (n_gy, L), 0)
    wall = wm[...]
    recip = 1.0 / wall

    def row_at(values, index):
        picked = jnp.sum(jnp.where(rid == index, values, 0.0), axis=0, keepdims=True)
        return jnp.broadcast_to(picked, (8, L))

    def whole(values):
        return jnp.sum(jnp.sum(values, axis=0, keepdims=True), axis=1, keepdims=True)

    total_h = whole(recip)
    below_h = whole(jnp.where(rid < gy, recip, 0.0))
    r_own, r_next, r_prev = row_at(recip, gy), row_at(recip, up_gy), row_at(recip, down_gy)
    wall_own = row_at(wall, gy)
    lane8 = lanes((8, L))
    run_own, run_next, run_prev = running(r_own), running(r_next), running(r_prev)
    sum_own = jnp.sum(r_own[0:1], axis=1, keepdims=True)
    sum_prev = jnp.sum(r_prev[0:1], axis=1, keepdims=True)
    frac = (below_h + (run_own - 0.5 * r_own)) / total_h
    frac_next = (below_h + sum_own + (run_next - 0.5 * r_next)) / total_h
    frac_prev = (below_h - sum_prev + (run_prev - 0.5 * r_prev)) / total_h
    rows[ROW_FRAC] = frac

    def slots(values, start):
        values = jnp.where(lane8 < 4, rolled(values, -start), 0.0)
        step = 4
        while step < L:
            values = values + rolled(values, step)
            step *= 2
        return values

    for n, (values, start) in enumerate(((frac, 0), (frac, L - 4), (frac_next, 0), (frac_prev, L - 4))):
        rows[ROW_SLOTS + n] = slots(values, start)
    place = gy * L + lane8
    last = n_gy * L
    within8 = lax.rem(lane8, 4)
    for k in range(7):
        entry = jnp.full((8, L), INTERIOR[k], F32)
        for row, table in ((0, ROW_FIRST), (1, ROW_SECOND), (2, ROW_THIRD), (last - 3, ROW_THIRD),
                           (last - 2, ROW_SECOND_LAST), (last - 1, ROW_LAST)):
            entry = jnp.where(place == row, table[k], entry)
        entry = entry * (0.5 * wall_own)
        reach = lane8 + (k - 3)
        rows[k] = jnp.where((reach >= 0) & (reach < L), entry, 0.0)
        d = k - 3
        if d > 0:
            rows[ROW_EDGES + d - 1] = jnp.where(within8 + d >= 4, slots(entry, L - 4), 0.0)
        if d < 0:
            rows[ROW_EDGES + 2 - d] = jnp.where(within8 + d < 0, slots(entry, 0), 0.0)
    r60 = r_own[0:1] * (1.0 / 60.0)

    first_row, second_row = sm[0:1, :], sm[1:2, :]
    own_m = jnp.where(gx == 0, first_row, second_row)
    other_m = jnp.where(gx == 0, second_row, first_row)
    own_cols = jnp.broadcast_to(own_m, (L, L)).T
    other_cols = jnp.broadcast_to(other_m, (L, L)).T
    m_wide[0:HALO, :] = other_cols[L - HALO:L, :]
    m_wide[HALO:HALO + L, :] = own_cols
    m_wide[HALO + L:WIDE, :] = other_cols[0:HALO, :]
    m120[...] = own_cols * (1.0 / 120.0)

    pl.semaphore_wait(barrier, count)

    gx_copies = []
    for f in range(2):
        for side, (src, dst) in enumerate(((L - HALO, 0), (0, HALO + L))):
            gx_copies.append(pltpu.make_async_remote_copy(
                src_ref=vel.at[f, :, pl.ds(src, HALO)], dst_ref=uw.at[f, :, pl.ds(dst, HALO)],
                send_sem=gx_send.at[f, side], recv_sem=gx_recv.at[f, side],
                device_id={"gx": other}, device_id_type=MESH))
            gx_copies[-1].start()

    for copy in loads:
        copy.wait()

    def pack_field(read, out, extent):
        for x0, size in chunks(extent, 32):
            slot = lanes((size, L)) // 4

            def body(z, carry):
                front, back = carry
                value = read(z, x0, size)
                mine = slot == z
                front = jnp.where(mine, pltpu.roll(value, 4 * z, 1), front)
                back = jnp.where(mine, pltpu.roll(value, lax.rem(4 * z + 4, L), 1), back)
                return front, back

            zero = jnp.zeros((size, L), F32)
            front, back = lax.fori_loop(0, depth, body, (zero, zero))
            out(0, x0, size, front)
            out(1, x0, size, back)

    for f in range(2):
        def store(side, x0, size, value, f=f):
            pack[side, f, pl.ds(x0, size), :] = value

        pack_field(lambda z, x0, size, f=f: uw[f, z, pl.ds(HALO + x0, size), :], store, L)

    y_copies = []
    for side, target in ((0, down_gy), (1, up_gy)):
        y_copies.append(pltpu.make_async_remote_copy(
            src_ref=pack.at[side], dst_ref=halo.at[side],
            send_sem=y_send.at[0, side], recv_sem=y_recv.at[0, side],
            device_id={"gy": target}, device_id_type=MESH))
        y_copies[-1].start()

    for copy in gx_copies:
        copy.wait()

    lane_small = lanes((8, L))
    shift = HALO - EDGE

    def around(z, d):
        return lax.rem(z + (depth + d), depth)

    def slope_plane(z, sums):
        sums = list(sums)
        for x0, size in chunks(SPAN, 32):
            du = slope_sum(lambda d: uw[0, z, pl.ds(shift + x0 + d, size), :])
            dw = slope_sum(lambda d: uw[1, around(z, d), pl.ds(shift + x0, size), :])
            value = (m_wide[pl.ds(shift + x0, size), :] * du + dw) * r60
            slope[z, pl.ds(x0, size), :] = value
            line = jnp.sum(value, axis=1, keepdims=True)
            for t in range(size // 8):
                tile = x0 // 8 + t
                group, quarter = tile // 4, tile % 4
                sums[group] = jnp.where(lane_small == 32 * quarter + z, line[8 * t:8 * t + 8], sums[group])
        return tuple(sums)

    sums = lax.fori_loop(0, depth, slope_plane, tuple(jnp.zeros((8, L), F32) for _ in range(GROUPS)))
    own = jnp.concatenate(sums, axis=0)

    def send_stage(stage):
        stride, size = rings[stage]
        copies = []
        for o in range(1, size):
            copies.append(pltpu.make_async_remote_copy(
                src_ref=stage_out.at[stage], dst_ref=stage_in.at[stage, o - 1],
                send_sem=st_send.at[stage, o - 1], recv_sem=st_recv.at[stage, o - 1],
                device_id={"gy": peer(stride, size, o)}, device_id_type=MESH))
            copies[-1].start()
        return copies

    def plane_terms(z, carry):
        for x0, size in chunks(L, 32):
            def at(f):
                return lambda d: uw[f, z, pl.ds(HALO + x0 + d, size), :]

            def over(f):
                return lambda d: uw[f, around(z, d), pl.ds(HALO + x0, size), :]

            along_x = skew(at(0), (at(0), at(1)))
            along_z = skew(over(1), (over(0), over(1)))
            m = m120[pl.ds(x0, size), :]
            for f in range(2):
                part[f, z, pl.ds(x0, size), :] = m * along_x[f] + along_z[f] * (1.0 / 120.0)
        return carry

    def running_plane(z, carry):
        for x0, size in chunks(SPAN, 32):
            value = slope[z, pl.ds(x0, size), :]
            crow[z, pl.ds(x0, size), :] = running(value) - 0.5 * value
        return carry

    def slope_pack():
        def store(side, x0, size, value):
            spack[side, pl.ds(x0, size), :] = value

        pack_field(lambda z, x0, size: slope[z, pl.ds(x0, size), :], store, SPAN)
        for side, target in ((0, down_gy), (1, up_gy)):
            y_copies.append(pltpu.make_async_remote_copy(
                src_ref=spack.at[side], dst_ref=sland.at[side],
                send_sem=y_send.at[1, side], recv_sem=y_recv.at[1, side],
                device_id={"gy": target}, device_id_type=MESH))
            y_copies[-1].start()
        for x0, size in chunks(SPAN, 32):
            slot = lanes((size, L)) // 4

            def body(z, carry):
                line = jnp.sum(slope[z, pl.ds(x0, size), :], axis=1, keepdims=True)
                return jnp.where(slot == z, line, carry)

            tot_pack[pl.ds(x0, size), :] = lax.fori_loop(0, depth, body, jnp.zeros((size, L), F32))

    def work(stage):
        if stage == 0:
            slope_pack()
            lax.fori_loop(0, depth, running_plane, 0)
        cut = [0] + [depth * k // len(rings) for k in range(1, len(rings))] + [depth]
        lax.fori_loop(cut[stage], cut[stage + 1], plane_terms, 0)

    below = jnp.zeros((8 * GROUPS, L), F32)
    for stage, (stride, size) in enumerate(rings):
        stage_out[stage] = own
        copies = send_stage(stage)
        work(stage)
        mine = lax.rem(gy // stride, size)
        for copy in copies:
            copy.wait()
        own = stage_out[stage]
        for o in range(1, size):
            sender = lax.rem(mine + size - o, size)
            value = stage_in[stage, o - 1]
            own = own + value
            below = below + jnp.where(sender < mine, value, 0.0)
        if stage < len(rings) - 1:
            below_total[0] = below
            below = below_total[0]
    below_total[0] = below
    below_total[1] = own

    for copy in y_copies:
        copy.wait()
    for x0, size in chunks(SPAN, 32):
        within = lax.rem(lanes((size, L)), 4)
        own_rows = pl.ds(x0, size)
        total_line = tot_pack[own_rows, :]

        def from_start(values):
            result = 0.5 * values
            for k in range(1, 4):
                result = result + jnp.where(within >= k, rolled(values, k), 0.0)
            return result

        def to_end(values):
            result = 0.5 * values
            for k in range(1, 4):
                result = result + jnp.where(within <= 3 - k, rolled(values, -k), 0.0)
            return result

        chalo[FRONT, own_rows, :] = from_start(spack[0, own_rows, :])
        chalo[BACK, own_rows, :] = total_line - to_end(spack[1, own_rows, :])
        chalo[NEXT, own_rows, :] = total_line + from_start(sland[0, own_rows, :])
        chalo[PREV, own_rows, :] = -to_end(sland[1, own_rows, :])


def second_kernel(
    depth, uw, crow, halo, chalo, part, below_total, rows, m120,
    out, vel, result, vslots, edges, out_sem,
):
    frac = rows[ROW_FRAC][0:1]

    def around(z, d):
        return lax.rem(z + (depth + d), depth)

    lane_from = lax.broadcasted_iota(jnp.int32, (L, L), 0)
    plane_to = lanes((L, L)) // 4
    both = below_total[...].reshape(2 * 8 * GROUPS, L)
    for quarter in range(4):
        pick = (lane_from == 32 * quarter + plane_to).astype(F32)
        spread = jnp.dot(both, pick, precision=lax.Precision.HIGHEST, preferred_element_type=F32)
        for group in range(GROUPS):
            tile = 4 * group + quarter
            if tile >= TILES:
                continue
            rows_of = pl.ds(8 * tile, 8)
            below = spread[8 * group:8 * group + 8]
            total = spread[8 * (GROUPS + group):8 * (GROUPS + group) + 8]
            for n in range(4):
                vslots[n, rows_of, :] = rows[ROW_SLOTS + n] * total - (chalo[n, rows_of, :] + below)

    for x0, size in chunks(L, 32):
        own, own_v = pl.ds(x0, size), pl.ds(EDGE + x0, size)
        for side, here, there, first in ((0, FRONT, PREV, 3), (1, BACK, NEXT, 0)):
            centre = vslots[here, own_v, :]
            away = [halo[1 - side, 0, own, :], vslots[there, own_v, :], halo[1 - side, 1, own, :]]
            sums = [None] * 3
            for d in range(1, 4):
                near = [rolled(x, 4 - d if side else d - 4) for x in away]
                factor = rows[ROW_EDGES + first + d - 1][0:1] * (centre + near[1])
                for f in range(3):
                    term = factor * near[f]
                    sums[f] = term if sums[f] is None else sums[f] + term
            for f in range(3):
                edges[side, f, own, :] = sums[f]

    def column(which, z, x0, size):
        pieces = []
        for t in range(size // 8):
            tile = x0 // 8 + t
            group, quarter = tile // 4, tile % 4
            values = below_total[which, pl.ds(8 * group, 8), :]
            turned = pltpu.roll(values, lax.rem(2 * L - 32 * quarter - z, L), 1)
            pieces.append(jnp.broadcast_to(turned[:, 0:1], (8, L)))
        return jnp.concatenate(pieces, axis=0)

    def normal_plane(z, carry):
        for x0, size in chunks(SPAN, 32):
            own = pl.ds(x0, size)
            below, total = column(0, z, x0, size), column(1, z, x0, size)
            vel[z, own, :] = frac * total - (crow[z, own, :] + below)
        return carry

    lax.fori_loop(0, depth, normal_plane, 0)

    def plane(z, carry):
        to_front, to_back = lax.rem(L - 4 * z, L), lax.rem(2 * L - 4 - 4 * z, L)
        for x0, size in chunks(L, STEP):
            lane = lanes((size, L))
            own = pl.ds(x0, size)

            def at(d):
                return vel[z, pl.ds(EDGE + x0 + d, size), :]

            def over(d):
                return vel[around(z, d), pl.ds(EDGE + x0, size), :]

            def q_at(d):
                return uw[0, z, pl.ds(HALO + x0 + d, size), :]

            def q_over(d):
                return uw[1, around(z, d), pl.ds(HALO + x0, size), :]

            (along_x,) = skew(q_at, (at,))
            (along_z,) = skew(q_over, (over,))
            sums = [part[0, z, own, :], m120[own, :] * along_x + along_z * (1.0 / 120.0), part[1, z, own, :]]
            fields = [q_at(0), at(0), q_over(0)]
            for k in range(7):
                near = [rolled(x, 3 - k) for x in fields]
                factor = rows[k][0:1] * (fields[1] + near[1])
                for f in range(3):
                    sums[f] = sums[f] + factor * near[f]
            for f in range(3):
                edge = jnp.where(lane >= L - 4, pltpu.roll(edges[1, f, own, :], to_back, 1), 0.0)
                edge = jnp.where(lane < 4, pltpu.roll(edges[0, f, own, :], to_front, 1), edge)
                result[z, f, own, :] = sums[f] + edge
        pltpu.make_async_copy(result.at[z], out.at[:, z], out_sem.at[z]).start()
        return carry

    lax.fori_loop(0, depth, plane, 0)

    def finish(z, carry):
        pltpu.make_async_copy(result.at[z], out.at[:, z], out_sem.at[z]).wait()
        return carry

    lax.fori_loop(0, depth, finish, 0)


def shards(n_gy, velocity, stream_metric, wall_metric):
    depth = velocity.shape[1]
    n_ring = len(rings_of(n_gy))
    others = max(size for _, size in rings_of(n_gy)) - 1
    kept = [
        (2, depth, WIDE, L),
        (depth, SPAN, L),
        (2, 2, L, L),
        (4, SPAN, L),
        (2, depth, L, L),
        (2, 8 * GROUPS, L),
        (ROWS, 8, L),
        (L, L),
    ]
    here = pl.BlockSpec(memory_space=pltpu.VMEM)
    anywhere = pl.BlockSpec(memory_space=pl.ANY)
    dma = pltpu.SemaphoreType.DMA
    held = pl.pallas_call(
        functools.partial(first_kernel, n_gy, depth),
        out_shape=[KEEP(shape) for shape in kept],
        in_specs=[pl.BlockSpec(memory_space=pltpu.HBM), here, here],
        out_specs=[here] * len(kept),
        scratch_shapes=[
            pltpu.VMEM((depth, SPAN, L), F32),
            pltpu.VMEM((WIDE, L), F32),
            pltpu.VMEM((2, 2, L, L), F32),
            pltpu.VMEM((2, SPAN, L), F32),
            pltpu.VMEM((2, SPAN, L), F32),
            pltpu.VMEM((n_ring, 8 * GROUPS, L), F32),
            pltpu.VMEM((n_ring, others, 8 * GROUPS, L), F32),
            pltpu.VMEM((SPAN, L), F32),
            dma((2, 2)), dma((2, 2)), dma((2, 2)), dma((2, 2)), dma((2, 2)),
            dma((n_ring, others)), dma((n_ring, others)),
        ],
        compiler_params=pltpu.CompilerParams(
            collective_id=0, has_side_effects=True, vmem_limit_bytes=VMEM_FIRST),
        name="exchange",
    )(velocity, stream_metric.reshape(2, L), wall_metric.reshape(n_gy, L))
    return pl.pallas_call(
        functools.partial(second_kernel, depth),
        out_shape=jax.ShapeDtypeStruct((3, depth, L, L), F32),
        in_specs=[here] * len(kept),
        out_specs=anywhere,
        scratch_shapes=[
            pltpu.VMEM((depth, SPAN, L), F32),
            pltpu.VMEM((depth, 3, L, L), F32),
            pltpu.VMEM((4, SPAN, L), F32),
            pltpu.VMEM((2, 3, L, L), F32),
            dma((depth,)),
        ],
        compiler_params=pltpu.CompilerParams(vmem_limit_bytes=VMEM_SECOND),
        name="advect",
    )(*held)


STEP = 32
VMEM_FIRST = 16 * 2**20
VMEM_SECOND = 20 * 2**20


def KEEP(shape):
    return jax.ShapeDtypeStruct(shape, F32)


def solution(mesh):
    spec = P(None, None, "gx", "gy")
    return jax.shard_map(
        functools.partial(shards, mesh.shape["gy"]), mesh=mesh,
        in_specs=(spec, P(), P()), out_specs=spec, check_vma=False)
```

profile of v0, /device:TPU:0, one launch (start us, length us, event | category | flops | bytes accessed | tf_op | source)
XLA Modules:
  0.0 111.6 jit_solution(15685458643674755454)
XLA Ops:
  0.0 0.0 copy-start
  0.0 2.2 %copy-done = f32[2,32,128,128]{3,2,1,0:T(8,128)S(1)} copy-done((f32[2,32,128,128]{3,2,1,0:T(8,128)S(1)}, f32[2,32,128,128]{3,2,1,0:T(8,128)}, u32[]{:S(2)}) %copy-start) | copy-done | bytes 4194328
  2.2 0.0 copy-start.1
  2.2 0.8 copy-done.1
  2.9 0.0 copy-start.2
  2.9 0.7 copy-done.2
  3.6 83.0 %exchange.1 = (f32[2,32,144,128]{3,2,1,0:T(8,128)S(1)}, f32[32,136,128]{2,1,0:T(8,128)S(1)}, f32[2,2,128,128]{3,2,1,0:T(8,128)S(1)}, f32[4,136,128]{2,1,0:T(8,12...) custom-call(f32[2,32,128,128]{3,2,1,0:T(8,128)S(1)} %copy-done, ...), custom_call_target="tpu_custom_call" | custom-call | tf_op jit(solution)/shard_map/exchange/pallas_call | solution.py:480
  86.7 24.9 %advect.1 = f32[3,32,128,128]{3,2,1,0:T(8,128)} custom-call(f32[2,32,144,128]{3,2,1,0:T(8,128)S(1)} %get-tuple-element.13.uw, f32[32,136,128]{2,1,0:T(8,128)S(1)} %get-tuple-element.14.crow, f32[2,2,128,128]{3,2,1,0:T(8,128)S(1)} %get-tuple-element.15.halo, f32[4,136,128]{2,1,0:T(8,128)S(1)} %get-tuple-element.16.chalo, ...), custom_call_target="tpu_custom_call" | custom-call | tf_op jit(solution)/shard_map/advect/pallas_call | solution.py:501
Async XLA Ops:
  0.0 2.2 %copy-start = (f32[2,32,128,128]{3,2,1,0:T(8,128)S(1)}, f32[2,32,128,128]{3,2,1,0:T(8,128)}, u32[]{:S(2)}) copy-start(f32[2,32,128,128]{3,2,1,0:T(8,128)} %vel.1) | copy-start | bytes 12582916
  2.2 0.8 copy-start.1
  2.9 0.7 copy-start.2
where the time goes:
time: 112 us
  Pallas kernels  108 us (96%)
  local copies, waits for them, and re-layouts  3.62 us (3%)
    pallas_call x1, Pallas kernels, shards(): pl.pallas_call(functools.partial(first_kernel, n_gy, depth), out_shape=[K...  83 us
    pallas_call x1, Pallas kernels, shards(): pl.pallas_call(functools.partial(second_kernel, depth), out_shape=jax.Sha...  24.9 us
    unnamed x6, local copies, waits for them, and re-layouts  3.62 us

commit v1 on v0

v1 whole, which is shorter than its diff:
```python
import functools

import jax
import jax.numpy as jnp
from jax import lax
from jax.experimental import pallas as pl
from jax.experimental.pallas import tpu as pltpu
from jax.sharding import PartitionSpec as P

MESH = pl.DeviceIdType.MESH
F32, BF16 = jnp.float32, jnp.bfloat16
L = 128
HALO = 8
EDGE = 4
WIDE = L + 2 * HALO
SPAN = L + 2 * EDGE
CENTRAL = (45.0, -9.0, 1.0)
INTERIOR = (-1.0, 9.0, -45.0, 0.0, 45.0, -9.0, 1.0)
ROW_FIRST = (0.0, 0.0, 0.0, -110.0, 180.0, -90.0, 20.0)
ROW_SECOND = (0.0, 0.0, -20.0, -30.0, 60.0, -10.0, 0.0)
ROW_THIRD = (0.0, 5.0, -40.0, 0.0, 40.0, -5.0, 0.0)
ROW_SECOND_LAST = (0.0, 10.0, -60.0, 30.0, 20.0, 0.0, 0.0)
ROW_LAST = (-20.0, 90.0, -180.0, 110.0, 0.0, 0.0, 0.0)
TILES = SPAN // 8
GROUPS = -(-TILES // 4)
PACKED = 8 * GROUPS
SLOT, HALF = 8, 16
ROW_FRAC, ROW_SCALE, ROW_OWN, ROW_AWAY, ROW_AFTER, ROW_BEFORE, ROWS = 7, 8, 9, 10, 11, 14, 17


def rings_of(count):
    size = 4 if count % 4 == 0 and count > 16 else 2
    rings, stride = [], 1
    while stride < count:
        rings.append((stride, size))
        stride *= size
    return rings


def lanes(shape):
    return lax.broadcasted_iota(jnp.int32, shape, len(shape) - 1)


def rolled(x, shift):
    if isinstance(shift, int):
        shift %= L
        if shift == 0:
            return x
    return pltpu.roll(x, shift, len(x.shape) - 1)


def running(x):
    lane = lanes(x.shape)
    step = 1
    while step < L:
        x = x + jnp.where(lane >= step, rolled(x, step), 0.0)
        step *= 2
    return x


def scaled(x, weight):
    return x if weight == 1.0 else x * weight


def chunks(total, size):
    return [(min(i, total - size), size) for i in range(0, total, size)]


def pieces(x):
    high = x.astype(BF16)
    rest = x - high.astype(F32)
    middle = rest.astype(BF16)
    low = (rest - middle.astype(F32)).astype(BF16)
    return jnp.concatenate([high, middle, low], axis=1)


def skew(adv, fields):
    centre = adv(0)
    sums = [None] * len(fields)
    for d, weight in enumerate(CENTRAL, start=1):
        up = scaled(centre + adv(d), weight)
        down = scaled(centre + adv(-d), weight)
        for n, field in enumerate(fields):
            term = up * field(d) - down * field(-d)
            sums[n] = term if sums[n] is None else sums[n] + term
    return sums


def slope_sum(field):
    total = None
    for d, weight in enumerate(CENTRAL, start=1):
        term = scaled(field(d) - field(-d), weight)
        total = term if total is None else total + term
    return total


def first_kernel(
    n_gy, depth,
    vel, sm_far, wm_far,
    uw, crow, halo, shalo, part, lines, rows, m120,
    slope, m_wide, ladder, stage_out, stage_in, sm, wm, left_even, left_odd,
    load_sem, gx_send, gx_recv, y_send, y_recv, st_send, st_recv,
):
    gx, gy = lax.axis_index("gx"), lax.axis_index("gy")
    other = 1 - gx
    rings = rings_of(n_gy)
    up_gy, down_gy = lax.rem(gy + 1, n_gy), lax.rem(gy + n_gy - 1, n_gy)
    half = min(HALF, depth)
    halves = depth // half

    def peer(stride, size, offset):
        place = lax.rem(gy // stride, size)
        return gy + (lax.rem(place + offset, size) - place) * stride

    small = [pltpu.make_async_copy(sm_far, sm, load_sem.at[2]), pltpu.make_async_copy(wm_far, wm, load_sem.at[3])]
    for copy in small:
        copy.start()
    loads = []
    for f in range(2):
        loads.append(pltpu.make_async_copy(vel.at[f], uw.at[f, :, pl.ds(HALO, L)], load_sem.at[f]))
        loads[-1].start()

    barrier = pltpu.get_barrier_semaphore()
    count = 0
    targets = [{"gx": other}, {"gy": up_gy}, {"gy": down_gy}]
    for stride, size in rings:
        targets += [{"gy": peer(stride, size, o)} for o in range(1, size)]
    for target in targets:
        pl.semaphore_signal(barrier, inc=1, device_id=target, device_id_type=MESH)
        count += 1

    for copy in small:
        copy.wait()
    rid = lax.broadcasted_iota(jnp.int32, (n_gy, L), 0)
    wall = wm[...]
    recip = 1.0 / wall

    def row_at(values, index):
        picked = jnp.sum(jnp.where(rid == index, values, 0.0), axis=0, keepdims=True)
        return jnp.broadcast_to(picked, (8, L))

    def whole(values):
        return jnp.sum(jnp.sum(values, axis=0, keepdims=True), axis=1, keepdims=True)

    total_h = whole(recip)
    below_h = whole(jnp.where(rid < gy, recip, 0.0))
    r_own, r_next, r_prev = row_at(recip, gy), row_at(recip, up_gy), row_at(recip, down_gy)
    wall_own = row_at(wall, gy)
    lane8 = lanes((8, L))
    run_own, run_next, run_prev = running(r_own), running(r_next), running(r_prev)
    sum_own = jnp.sum(r_own[0:1], axis=1, keepdims=True)
    sum_prev = jnp.sum(r_prev[0:1], axis=1, keepdims=True)
    frac = (below_h + (run_own - 0.5 * r_own)) / total_h
    frac_next = (below_h + sum_own + (run_next - 0.5 * r_next)) / total_h
    frac_prev = (below_h - sum_prev + (run_prev - 0.5 * r_prev)) / total_h
    scale = wall_own * (1.0 / 120.0)
    rows[ROW_FRAC] = frac
    rows[ROW_SCALE] = scale
    within8 = lax.rem(lane8, SLOT)

    def slots(last, first):
        values = jnp.where(lane8 < 4, rolled(last, 4), 0.0)
        values = values + jnp.where((lane8 >= 4) & (lane8 < 8), rolled(first, 4), 0.0)
        step = SLOT
        while step < L:
            values = values + rolled(values, step)
            step *= 2
        return values

    rows[ROW_OWN] = slots(frac, frac)
    rows[ROW_AWAY] = slots(frac_prev, frac_next)
    place = gy * L + lane8
    last_row = n_gy * L - 1
    for k in range(7):
        entry = jnp.full((8, L), INTERIOR[k], F32)
        for row, table in ((0, ROW_FIRST), (1, ROW_SECOND), (2, ROW_THIRD), (last_row - 2, ROW_THIRD),
                           (last_row - 1, ROW_SECOND_LAST), (last_row, ROW_LAST)):
            entry = jnp.where(place == row, table[k], entry)
        rows[k] = entry
        d = k - 3
        if d != 0:
            both = slots(entry * scale, entry * scale)
        if d > 0:
            rows[ROW_AFTER + d - 1] = jnp.where((within8 < 4) & (within8 + d >= 4), both, 0.0)
        if d < 0:
            rows[ROW_BEFORE - d - 1] = jnp.where((within8 >= 4) & (within8 + d < 4), both, 0.0)
    r60 = r_own[0:1] * (1.0 / 60.0)

    first_row, second_row = sm[0:1, :], sm[1:2, :]
    own_m = jnp.where(gx == 0, first_row, second_row)
    other_m = jnp.where(gx == 0, second_row, first_row)
    own_cols = jnp.broadcast_to(own_m, (L, L)).T
    other_cols = jnp.broadcast_to(other_m, (L, L)).T
    m_wide[0:HALO, :] = other_cols[L - HALO:L, :]
    m_wide[HALO:HALO + L, :] = own_cols
    m_wide[HALO + L:WIDE, :] = other_cols[0:HALO, :]
    m120[...] = own_cols * (1.0 / 120.0)
    source = lax.broadcasted_iota(jnp.int32, (L, 2 * L), 0)
    target = lanes((L, 2 * L))
    steps = jnp.where(source < target, 1.0, jnp.where(source == target, 0.5, 0.0)).astype(BF16)
    for n in range(3):
        ladder[n * L:(n + 1) * L, :] = steps

    pl.semaphore_wait(barrier, count)

    gx_copies = []
    for f in range(2):
        for side, (src, dst) in enumerate(((L - HALO, 0), (0, HALO + L))):
            gx_copies.append(pltpu.make_async_remote_copy(
                src_ref=vel.at[f, :, pl.ds(src, HALO)], dst_ref=uw.at[f, :, pl.ds(dst, HALO)],
                send_sem=gx_send.at[f, side], recv_sem=gx_recv.at[f, side],
                device_id={"gx": other}, device_id_type=MESH))
            gx_copies[-1].start()

    for copy in loads:
        copy.wait()

    def send_slots(array, n):
        copies = []
        for side, where in ((1, down_gy), (2, up_gy)):
            copies.append(pltpu.make_async_remote_copy(
                src_ref=array.at[0], dst_ref=array.at[side],
                send_sem=y_send.at[n, side - 1], recv_sem=y_recv.at[n, side - 1],
                device_id={"gy": where}, device_id_type=MESH))
            copies[-1].start()
        return copies

    def pack(read, extent, store):
        slot = lanes((extent, L)) // SLOT
        for h in range(halves):
            def body(z, packed):
                return jnp.where(slot == z, pltpu.roll(read(h * half + z), SLOT * z + 4, 1), packed)

            store(h, lax.fori_loop(0, half, body, jnp.zeros((extent, L), F32), unroll=4))

    for f in range(2):
        def store_halo(h, value, f=f):
            halo[0, f, h] = value

        pack(lambda z, f=f: uw[f, z, pl.ds(HALO, L), :], L, store_halo)
    y_copies = send_slots(halo, 0)

    for copy in gx_copies:
        copy.wait()

    lane_small = lanes((8, L))
    shift = HALO - EDGE

    def around(z, d):
        return lax.rem(z + (depth + d), depth)

    def slope_split(z, left):
        for x0, size in chunks(SPAN, 48):
            du = slope_sum(lambda d: uw[0, z, pl.ds(shift + x0 + d, size), :])
            dw = slope_sum(lambda d: uw[1, around(z, d), pl.ds(shift + x0, size), :])
            value = (m_wide[pl.ds(shift + x0, size), :] * du + dw) * r60
            slope[z, pl.ds(x0, size), :] = value
            left[pl.ds(min(x0, SPAN - size) + (SLOT if x0 + size == SPAN else 0), size), :] = pieces(value)

    def row_in_left(row):
        return row if row < SPAN - 48 else row + SLOT

    def slope_climb(z, left, sums):
        climbed = jnp.dot(left[...], ladder[...], preferred_element_type=F32)
        for tile in range(TILES):
            row = row_in_left(8 * tile)
            crow[z, pl.ds(8 * tile, 8), :] = climbed[row:row + 8, :L]
            group, quarter = tile // 4, tile % 4
            sums[group] = jnp.where(lane_small == 32 * quarter + z, climbed[row:row + 8, L:], sums[group])
        return sums

    slope_split(0, left_even)

    def slope_plane(n, sums):
        z = 2 * n
        slope_split(z + 1, left_odd)
        sums = slope_climb(z, left_even, list(sums))
        slope_split(around(z, 2), left_even)
        return tuple(slope_climb(z + 1, left_odd, sums))

    sums = lax.fori_loop(0, depth // 2, slope_plane, tuple(jnp.zeros((8, L), F32) for _ in range(GROUPS)))
    own = jnp.concatenate(sums, axis=0)
    lines[2] = own

    def send_stage(stage):
        stride, size = rings[stage]
        copies = []
        for o in range(1, size):
            copies.append(pltpu.make_async_remote_copy(
                src_ref=stage_out.at[stage], dst_ref=stage_in.at[stage, o - 1],
                send_sem=st_send.at[stage, o - 1], recv_sem=st_recv.at[stage, o - 1],
                device_id={"gy": peer(stride, size, o)}, device_id_type=MESH))
            copies[-1].start()
        return copies

    def plane_terms(z, carry):
        for x0, size in chunks(L, 32):
            def at(f):
                return lambda d: uw[f, z, pl.ds(HALO + x0 + d, size), :]

            def over(f):
                return lambda d: uw[f, around(z, d), pl.ds(HALO + x0, size), :]

            along_x = skew(at(0), (at(0), at(1)))
            along_z = skew(over(1), (over(0), over(1)))
            m = m120[pl.ds(x0, size), :]
            for f in range(2):
                part[f, z, pl.ds(x0, size), :] = m * along_x[f] + along_z[f] * (1.0 / 120.0)
        return carry

    below = jnp.zeros((PACKED, L), F32)
    cut = [depth * k // len(rings) for k in range(len(rings) + 1)]
    for stage, (stride, size) in enumerate(rings):
        stage_out[stage] = own
        copies = send_stage(stage)
        if stage == 0:
            def store_slope(h, value):
                shalo[0, h] = value

            pack(lambda z: slope[z], SPAN, store_slope)
            y_copies += send_slots(shalo, 1)
        lax.fori_loop(cut[stage], cut[stage + 1], plane_terms, 0)
        mine = lax.rem(gy // stride, size)
        for copy in copies:
            copy.wait()
        own = stage_out[stage]
        for o in range(1, size):
            sender = lax.rem(mine + size - o, size)
            value = stage_in[stage, o - 1]
            own = own + value
            below = below + jnp.where(sender < mine, value, 0.0)
        if stage < len(rings) - 1:
            lines[0] = below
            below = lines[0]
    lines[0] = below
    lines[1] = own

    for copy in y_copies:
        copy.wait()


def second_kernel(
    depth, uw, crow, halo, shalo, part, lines, rows, m120,
    out, vel, result, spread, vslots, edges, picks, weights,
    left_even, left_odd, right_even, right_odd, out_sem,
):
    half = min(HALF, depth)
    halves = depth // half
    frac = rows[ROW_FRAC][0:1]
    scale = rows[ROW_SCALE][0:1]

    def around(z, d):
        return lax.rem(z + (depth + d), depth)

    source = lax.broadcasted_iota(jnp.int32, (L, L), 0)
    target = lanes((L, L))
    stencil = jnp.zeros((L, L), F32)
    for k in range(7):
        stencil = jnp.where(source - target == k - 3, rows[k][0:1], stencil)
    stencil = stencil.astype(BF16)
    for n in range(3):
        weights[n * L:(n + 1) * L, :] = stencil

    packed = pieces(lines[...].reshape(3 * PACKED, L))
    for quarter in range(4):
        for h in range(halves):
            pick = (source == 32 * quarter + half * h + target // SLOT).astype(F32).astype(BF16)
            for n in range(3):
                picks[n * L:(n + 1) * L, :] = pick
            found = jnp.dot(packed, picks[...], preferred_element_type=F32)
            for group in range(GROUPS):
                tile = 4 * group + quarter
                if tile < TILES:
                    for n in range(3):
                        at = n * PACKED + 8 * group
                        spread[n, h, pl.ds(8 * tile, 8), :] = found[at:at + 8]

    for h in range(halves):
        for x0, size in chunks(SPAN, 8 * 17):
            area = pl.ds(x0, size)
            within = lax.rem(lanes((size, L)), SLOT)
            first_rows = within >= 4
            below, total, line = (spread[n, h, area, :] for n in range(3))

            def local(values):
                result = 0.5 * values
                for k in range(1, 4):
                    result = result + jnp.where(within >= 4 + k, rolled(values, k), 0.0)
                    result = result + jnp.where(within <= 3 - k, rolled(values, -k), 0.0)
                return result

            near = local(shalo[0, h, area, :])
            away = local(jnp.where(first_rows, shalo[1, h, area, :], shalo[2, h, area, :]))
            near = jnp.where(first_rows, near, line - near)
            away = jnp.where(first_rows, line + away, -away)
            vslots[0, h, area, :] = rows[ROW_OWN][0:1] * total - (near + below)
            vslots[1, h, area, :] = rows[ROW_AWAY][0:1] * total - (away + below)

    for h in range(halves):
        for x0, size in chunks(L, 32):
            area, area_v = pl.ds(x0, size), pl.ds(EDGE + x0, size)
            first_rows = lax.rem(lanes((size, L)), SLOT) >= 4
            centre = vslots[0, h, area_v, :]
            away = [jnp.where(first_rows, halo[1, f, h, area, :], halo[2, f, h, area, :]) for f in range(2)]
            away = [away[0], vslots[1, h, area_v, :], away[1]]
            sums = [None] * 3
            for d in range(1, 4):
                for row, turn in ((ROW_AFTER, -d), (ROW_BEFORE, d)):
                    near = [rolled(x, turn) for x in away]
                    factor = rows[row + d - 1][0:1] * (centre + near[1])
                    for f in range(3):
                        term = factor * near[f]
                        sums[f] = term if sums[f] is None else sums[f] + term
            for f in range(3):
                edges[h, f, area, :] = sums[f]

    def normal_plane(z, carry):
        turn = lax.rem(L - z, L)
        turned = [[pltpu.roll(lines[n, pl.ds(8 * g, 8), :], turn, 1) for g in range(GROUPS)] for n in range(2)]
        for tile in range(TILES):
            group, at = tile // 4, 32 * (tile % 4)
            below, total = (jnp.broadcast_to(turned[n][group][:, at:at + 1], (8, L)) for n in range(2))
            area = pl.ds(8 * tile, 8)
            vel[z, area, :] = frac * total - (crow[z, area, :] + below)
        return carry

    lax.fori_loop(0, depth, normal_plane, 0, unroll=2)

    def at(z, x0, d):
        return vel[z, pl.ds(EDGE + x0 + d, STEP), :]

    def q_at(f, z, x0, d):
        return uw[f, z, pl.ds(HALO + x0 + d, STEP), :]

    def split(z, left):
        for x0 in range(0, L, STEP):
            v = at(z, x0, 0)
            for f, field in enumerate((q_at(0, z, x0, 0), v, q_at(1, z, x0, 0))):
                left[pl.ds(f * L + x0, STEP), :] = pieces(field)
                left[pl.ds((3 + f) * L + x0, STEP), :] = pieces(v * field)

    def plane(z, left, right, later):
        turn = lax.rem(2 * L - 4 - SLOT * lax.rem(z, half), L)
        right[...] = jnp.dot(left[...], weights[...], preferred_element_type=F32)
        if later is not None:
            split(*later)
        for x0 in range(0, L, STEP):
            own = pl.ds(x0, STEP)
            (along_x,) = skew(lambda d: q_at(0, z, x0, d), (lambda d: at(z, x0, d),))
            (along_z,) = skew(lambda d: q_at(1, around(z, d), x0, 0), (lambda d: at(around(z, d), x0, 0),))
            result[z, 1, own, :] = m120[own, :] * along_x + along_z * (1.0 / 120.0)
        for x0 in range(0, L, STEP):
            own = pl.ds(x0, STEP)
            lane = lanes((STEP, L))
            v = at(z, x0, 0)
            for f in range(3):
                others = result[z, 1, own, :] if f == 1 else part[f // 2, z, own, :]
                turned = pltpu.roll(edges[z // half, f, own, :], turn, 1)
                edge = jnp.where((lane < 4) | (lane >= L - 4), turned, 0.0)
                slope, flux = right[pl.ds(f * L + x0, STEP), :], right[pl.ds((3 + f) * L + x0, STEP), :]
                result[z, f, own, :] = others + (v * slope + flux) * scale + edge
        pltpu.make_async_copy(result.at[z], out.at[:, z], out_sem.at[z]).start()

    split(0, left_even)

    def two_planes(n, carry):
        z = 2 * n
        plane(z, left_even, right_even, (z + 1, left_odd))
        plane(z + 1, left_odd, right_odd, (around(z, 2), left_even))
        return carry

    lax.fori_loop(0, depth // 2, two_planes, 0)

    def finish(z, carry):
        pltpu.make_async_copy(result.at[z], out.at[:, z], out_sem.at[z]).wait()
        return carry

    lax.fori_loop(0, depth, finish, 0)


STEP = 32
VMEM_FIRST = 24 * 2**20
VMEM_SECOND = 24 * 2**20


def shards(n_gy, velocity, stream_metric, wall_metric):
    depth = velocity.shape[1]
    halves = depth // min(HALF, depth)
    n_ring = len(rings_of(n_gy))
    others = max(size for _, size in rings_of(n_gy)) - 1
    kept = [
        (2, depth, WIDE, L),
        (depth, SPAN, L),
        (3, 2, halves, L, L),
        (3, halves, SPAN, L),
        (2, depth, L, L),
        (3, PACKED, L),
        (ROWS, 8, L),
        (L, L),
    ]
    here = pl.BlockSpec(memory_space=pltpu.VMEM)
    anywhere = pl.BlockSpec(memory_space=pl.ANY)
    dma = pltpu.SemaphoreType.DMA
    held = pl.pallas_call(
        functools.partial(first_kernel, n_gy, depth),
        out_shape=[pltpu.VMEM(shape, F32) for shape in kept],
        in_specs=[pl.BlockSpec(memory_space=pltpu.HBM)] * 3,
        out_specs=[here] * len(kept),
        scratch_shapes=[
            pltpu.VMEM((depth, SPAN, L), F32),
            pltpu.VMEM((WIDE, L), F32),
            pltpu.VMEM((3 * L, 2 * L), BF16),
            pltpu.VMEM((n_ring, PACKED, L), F32),
            pltpu.VMEM((n_ring, others, PACKED, L), F32),
            pltpu.VMEM((2, L), F32),
            pltpu.VMEM((n_gy, L), F32),
            pltpu.VMEM((WIDE, 3 * L), BF16),
            pltpu.VMEM((WIDE, 3 * L), BF16),
            dma((4,)), dma((2, 2)), dma((2, 2)), dma((2, 2)), dma((2, 2)),
            dma((n_ring, others)), dma((n_ring, others)),
        ],
        compiler_params=pltpu.CompilerParams(
            collective_id=0, has_side_effects=True, vmem_limit_bytes=VMEM_FIRST),
        name="exchange",
    )(*(pltpu.with_memory_space_constraint(x, pltpu.HBM)
        for x in (velocity, stream_metric.reshape(2, L), wall_metric.reshape(n_gy, L))))
    return pl.pallas_call(
        functools.partial(second_kernel, depth),
        out_shape=jax.ShapeDtypeStruct((3, depth, L, L), F32),
        in_specs=[here] * len(kept),
        out_specs=anywhere,
        scratch_shapes=[
            pltpu.VMEM((depth, SPAN, L), F32),
            pltpu.VMEM((depth, 3, L, L), F32),
            pltpu.VMEM((3, halves, SPAN, L), F32),
            pltpu.VMEM((2, halves, SPAN, L), F32),
            pltpu.VMEM((halves, 3, L, L), F32),
            pltpu.VMEM((3 * L, L), BF16),
            pltpu.VMEM((3 * L, L), BF16),
            pltpu.VMEM((6 * L, 3 * L), BF16),
            pltpu.VMEM((6 * L, 3 * L), BF16),
            pltpu.VMEM((6 * L, L), F32),
            pltpu.VMEM((6 * L, L), F32),
            dma((depth,)),
        ],
        compiler_params=pltpu.CompilerParams(vmem_limit_bytes=VMEM_SECOND),
        name="advect",
    )(*held)


def solution(mesh):
    spec = P(None, None, "gx", "gy")
    return jax.shard_map(
        functools.partial(shards, mesh.shape["gy"]), mesh=mesh,
        in_specs=(spec, P(), P()), out_specs=spec, check_vma=False)
```

time: 112 us -> 46.7 us (0.42)
  Pallas kernels: 108 us -> 46.6 us
  local copies, waits for them, and re-layouts: 3.62 us -> 0 us
    pallas_call x1, Pallas kernels: 83 us -> 27.4 us  [shards(): pl.pallas_call(functools.partial(first_kernel, n_gy, depth), out_shape=[p...]
    pallas_call x1, Pallas kernels: 24.9 us -> 19.2 us  [shards(): pl.pallas_call(functools.partial(second_kernel, depth), out_shape=jax.Sha...]
    unnamed x6 -> x0, local copies, waits for them, and re-layouts: 3.62 us -> none
where the time goes in v1:
time: 46.7 us; the launch traced here: 46.6 us
  Pallas kernels  46.6 us (100%)
    pallas_call x1, Pallas kernels, shards(): pl.pallas_call(functools.partial(first_kernel, n_gy, depth), out_shape=[p...  27.4 us
    pallas_call x1, Pallas kernels, shards(): pl.pallas_call(functools.partial(second_kernel, depth), out_shape=jax.Sha...  19.2 us

profile of v1, /device:TPU:0, one launch (start us, length us, event | category | flops | bytes accessed | tf_op | source)
XLA Modules:
  0.0 46.6 jit_solution(15099184280860472868)
XLA Ops:
  0.0 27.4 %exchange.1 = (f32[2,32,144,128]{3,2,1,0:T(8,128)S(1)}, f32[32,136,128]{2,1,0:T(8,128)S(1)}, f32[3,2,2,128,128]{4,3,2,1,0:T(8,128)S(1)}, f32[3,2,136,128]{3,2,1,...) custom-call(f32[2,32,128,128]{3,2,1,0:T(8,128)} %vel.1, ...), custom_call_target="tpu_custom_call" | custom-call | tf_op jit(solution)/shard_map/exchange/pallas_call | solution.py:504
  27.4 19.2 %advect.1 = f32[3,32,128,128]{3,2,1,0:T(8,128)} custom-call(f32[2,32,144,128]{3,2,1,0:T(8,128)S(1)} %get-tuple-element.13.uw, f32[32,136,128]{2,1,0:T(8,128)S(1)} %get-tuple-element.14.crow, f32[3,2,2,128,128]{4,3,2,1,0:T(8,128)S(1)} %get-tuple-element.15.halo, f32[3,2,136,128]{3,2,1,0:T(8,128)S(1)} %get-tuple-element.16.shalo, ...), custom_call_target="tpu_custom_call" | custom-call | tf_op jit(solution)/shard_map/advect/pallas_call | solution.py:527

commit v2 on v1

--- a/solution.py
+++ b/solution.py
@@ -25,7 +25,7 @@
 GROUPS = -(-TILES // 4)
 PACKED = 8 * GROUPS
 SLOT, HALF = 8, 16
-ROW_FRAC, ROW_SCALE, ROW_OWN, ROW_AWAY, ROW_AFTER, ROW_BEFORE, ROWS = 7, 8, 9, 10, 11, 14, 17
+ROW_FRAC, ROW_SCALE, ROW_OWN, ROW_AWAY, ROW_SLOT, ROW_SLOT_SCALE, ROWS = 7, 8, 9, 10, 11, 18, 19
 
 
 def rings_of(count):
@@ -66,17 +66,31 @@
     return [(min(i, total - size), size) for i in range(0, total, size)]
 
 
-def pieces(x):
+def three(x):
     high = x.astype(BF16)
     rest = x - high.astype(F32)
     middle = rest.astype(BF16)
     low = (rest - middle.astype(F32)).astype(BF16)
-    return jnp.concatenate([high, middle, low], axis=1)
+    return high, middle, low
+
+
+def pieces(x):
+    return jnp.concatenate(three(x), axis=1)
+
+
+def pieces_of_two(x, y):
+    return jnp.concatenate([part for pair in zip(three(x), three(y)) for part in pair], axis=1)
 
 
 def skew(adv, fields):
     centre = adv(0)
     sums = [None] * len(fields)
+    if len(fields) == 1:
+        total = None
+        for d, weight in enumerate(CENTRAL, start=1):
+            term = (centre + adv(d)) * fields[0](d) - (centre + adv(-d)) * fields[0](-d)
+            total = scaled(term, weight) if total is None else total + scaled(term, weight)
+        return [total]
     for d, weight in enumerate(CENTRAL, start=1):
         up = scaled(centre + adv(d), weight)
         down = scaled(centre + adv(-d), weight)
@@ -156,7 +170,6 @@
     scale = wall_own * (1.0 / 120.0)
     rows[ROW_FRAC] = frac
     rows[ROW_SCALE] = scale
-    within8 = lax.rem(lane8, SLOT)
 
     def slots(last, first):
         values = jnp.where(lane8 < 4, rolled(last, 4), 0.0)
@@ -177,13 +190,8 @@
                            (last_row - 1, ROW_SECOND_LAST), (last_row, ROW_LAST)):
             entry = jnp.where(place == row, table[k], entry)
         rows[k] = entry
-        d = k - 3
-        if d != 0:
-            both = slots(entry * scale, entry * scale)
-        if d > 0:
-            rows[ROW_AFTER + d - 1] = jnp.where((within8 < 4) & (within8 + d >= 4), both, 0.0)
-        if d < 0:
-            rows[ROW_BEFORE - d - 1] = jnp.where((within8 >= 4) & (within8 + d < 4), both, 0.0)
+        rows[ROW_SLOT + k] = slots(entry, entry)
+    rows[ROW_SLOT_SCALE] = slots(scale, scale)
     r60 = r_own[0:1] * (1.0 / 60.0)
 
     first_row, second_row = sm[0:1, :], sm[1:2, :]
@@ -233,13 +241,6 @@
 
             store(h, lax.fori_loop(0, half, body, jnp.zeros((extent, L), F32), unroll=4))
 
-    for f in range(2):
-        def store_halo(h, value, f=f):
-            halo[0, f, h] = value
-
-        pack(lambda z, f=f: uw[f, z, pl.ds(HALO, L), :], L, store_halo)
-    y_copies = send_slots(halo, 0)
-
     for copy in gx_copies:
         copy.wait()
 
@@ -260,8 +261,9 @@
     def row_in_left(row):
         return row if row < SPAN - 48 else row + SLOT
 
-    def slope_climb(z, left, sums):
+    def slope_climb(z, left, sums, later):
         climbed = jnp.dot(left[...], ladder[...], preferred_element_type=F32)
+        slope_split(*later)
         for tile in range(TILES):
             row = row_in_left(8 * tile)
             crow[z, pl.ds(8 * tile, 8), :] = climbed[row:row + 8, :L]
@@ -273,10 +275,8 @@
 
     def slope_plane(n, sums):
         z = 2 * n
-        slope_split(z + 1, left_odd)
-        sums = slope_climb(z, left_even, list(sums))
-        slope_split(around(z, 2), left_even)
-        return tuple(slope_climb(z + 1, left_odd, sums))
+        sums = slope_climb(z, left_even, list(sums), (z + 1, left_odd))
+        return tuple(slope_climb(z + 1, left_odd, sums, (around(z, 2), left_even)))
 
     sums = lax.fori_loop(0, depth // 2, slope_plane, tuple(jnp.zeros((8, L), F32) for _ in range(GROUPS)))
     own = jnp.concatenate(sums, axis=0)
@@ -294,7 +294,7 @@
         return copies
 
     def plane_terms(z, carry):
-        for x0, size in chunks(L, 32):
+        for x0, size in chunks(L, 16):
             def at(f):
                 return lambda d: uw[f, z, pl.ds(HALO + x0 + d, size), :]
 
@@ -317,6 +317,12 @@
             def store_slope(h, value):
                 shalo[0, h] = value
 
+            for f in range(2):
+                def store_halo(h, value, f=f):
+                    halo[0, f, h] = value
+
+                pack(lambda z, f=f: uw[f, z, pl.ds(HALO, L), :], L, store_halo)
+            y_copies = send_slots(halo, 0)
             pack(lambda z: slope[z], SPAN, store_slope)
             y_copies += send_slots(shalo, 1)
         lax.fori_loop(cut[stage], cut[stage + 1], plane_terms, 0)
@@ -341,7 +347,7 @@
 
 def second_kernel(
     depth, uw, crow, halo, shalo, part, lines, rows, m120,
-    out, vel, result, spread, vslots, edges, picks, weights,
+    out, vel, result, parts, vslots, edges, weights,
     left_even, left_odd, right_even, right_odd, out_sem,
 ):
     half = min(HALF, depth)
@@ -354,77 +360,94 @@
 
     source = lax.broadcasted_iota(jnp.int32, (L, L), 0)
     target = lanes((L, L))
+
+    def store_weights(ref, matrix):
+        matrix = matrix.astype(BF16)
+        nothing = jnp.zeros((L, L), BF16)
+        for n in range(3):
+            ref[2 * n * L:(2 * n + 1) * L, :] = jnp.concatenate([matrix, nothing], axis=1)
+            ref[(2 * n + 1) * L:(2 * n + 2) * L, :] = jnp.concatenate([nothing, matrix], axis=1)
+
+    packed = pieces(lines[...].reshape(3 * PACKED, L))
+    from_lane = lax.broadcasted_iota(jnp.int32, (3 * L, L), 0)
+    to_lane = lanes((3 * L, L))
+    for quarter in range(4):
+        pick = (from_lane // L == to_lane // 32) & (lax.rem(from_lane, L) == 32 * quarter + lax.rem(to_lane, 32))
+        found = jnp.dot(packed, pick.astype(F32).astype(BF16), preferred_element_type=F32)
+        for group in range(GROUPS):
+            tile = 4 * group + quarter
+            if tile < TILES:
+                for n in range(3):
+                    at = n * PACKED + 8 * group
+                    parts[n, pl.ds(8 * tile, 8), :] = found[at:at + 8]
+    for n in range(3):
+        parts[n, pl.ds(SPAN, 8), :] = jnp.zeros((8, L), F32)
+    source2 = lax.broadcasted_iota(jnp.int32, (L, halves * L), 0)
+    target2 = lanes((L, halves * L))
+    to_slot = (lax.rem(source2, 32) == half * (target2 // L) + lax.rem(target2, L) // SLOT) & (source2 < 96)
+    to_slot = to_slot.astype(F32).astype(BF16)
+
+    same_slot = source // SLOT == target // SLOT
+    place, aim = lax.rem(source, SLOT), lax.rem(target, SLOT)
+    passed = ((place >= 4) & (place < aim)) | ((place < 4) & (place > aim))
+    same_side = same_slot & ((place >= 4) == (aim >= 4))
+    local = jnp.where(same_side & passed, 1.0, jnp.where(source == target, 0.5, 0.0)).astype(BF16)
+    local = jnp.concatenate([local, local, local], axis=0)
+    first_rows = lax.rem(lanes((SPAN, L)), SLOT) >= 4
+    spread = [jnp.dot(parts[n].astype(BF16), to_slot, preferred_element_type=F32) for n in range(3)]
+    for h in range(halves):
+        below, total, line = (x[:SPAN, h * L:(h + 1) * L] for x in spread)
+        near = jnp.dot(pieces(shalo[0, h]), local, preferred_element_type=F32)
+        away = jnp.where(first_rows, shalo[1, h], shalo[2, h])
+        away = jnp.dot(pieces(away), local, preferred_element_type=F32)
+        near = jnp.where(first_rows, near, line - near)
+        away = jnp.where(first_rows, line + away, -away)
+        vslots[0, h] = rows[ROW_OWN][0:1] * total - (near + below)
+        vslots[1, h] = rows[ROW_AWAY][0:1] * total - (away + below)
+
+    across = same_slot & ((place >= 4) != (aim >= 4))
+    stencil = jnp.zeros((L, L), F32)
+    for k in range(7):
+        stencil = jnp.where(across & (source - target == k - 3), rows[ROW_SLOT + k][0:1], stencil)
+    store_weights(weights, stencil)
+    scale8 = rows[ROW_SLOT_SCALE][0:1]
+    for h in range(halves):
+        for x0, size in chunks(L, 32):
+            area = pl.ds(x0, size)
+            first = lax.rem(lanes((size, L)), SLOT) >= 4
+            v = vslots[1, h, pl.ds(EDGE + x0, size), :]
+            away = [jnp.where(first, halo[1, f, h, area, :], halo[2, f, h, area, :]) for f in range(2)]
+            for f, field in enumerate((away[0], v, away[1])):
+                left_even[pl.ds(f * L + x0, size), :] = pieces_of_two(field, v * field)
+        right_even[...] = jnp.dot(left_even[...], weights[...], preferred_element_type=F32)
+        for x0, size in chunks(L, 32):
+            v = vslots[0, h, pl.ds(EDGE + x0, size), :]
+            for f in range(3):
+                both = right_even[pl.ds(f * L + x0, size), :]
+                edges[h, f, pl.ds(x0, size), :] = (v * both[:, :L] + both[:, L:]) * scale8
+
     stencil = jnp.zeros((L, L), F32)
     for k in range(7):
         stencil = jnp.where(source - target == k - 3, rows[k][0:1], stencil)
-    stencil = stencil.astype(BF16)
-    for n in range(3):
-        weights[n * L:(n + 1) * L, :] = stencil
-
-    packed = pieces(lines[...].reshape(3 * PACKED, L))
-    for quarter in range(4):
-        for h in range(halves):
-            pick = (source == 32 * quarter + half * h + target // SLOT).astype(F32).astype(BF16)
-            for n in range(3):
-                picks[n * L:(n + 1) * L, :] = pick
-            found = jnp.dot(packed, picks[...], preferred_element_type=F32)
-            for group in range(GROUPS):
-                tile = 4 * group + quarter
-                if tile < TILES:
-                    for n in range(3):
-                        at = n * PACKED + 8 * group
-                        spread[n, h, pl.ds(8 * tile, 8), :] = found[at:at + 8]
-
-    for h in range(halves):
-        for x0, size in chunks(SPAN, 8 * 17):
-            area = pl.ds(x0, size)
-            within = lax.rem(lanes((size, L)), SLOT)
-            first_rows = within >= 4
-            below, total, line = (spread[n, h, area, :] for n in range(3))
-
-            def local(values):
-                result = 0.5 * values
-                for k in range(1, 4):
-                    result = result + jnp.where(within >= 4 + k, rolled(values, k), 0.0)
-                    result = result + jnp.where(within <= 3 - k, rolled(values, -k), 0.0)
-                return result
-
-            near = local(shalo[0, h, area, :])
-            away = local(jnp.where(first_rows, shalo[1, h, area, :], shalo[2, h, area, :]))
-            near = jnp.where(first_rows, near, line - near)
-            away = jnp.where(first_rows, line + away, -away)
-            vslots[0, h, area, :] = rows[ROW_OWN][0:1] * total - (near + below)
-            vslots[1, h, area, :] = rows[ROW_AWAY][0:1] * total - (away + below)
-
-    for h in range(halves):
-        for x0, size in chunks(L, 32):
-            area, area_v = pl.ds(x0, size), pl.ds(EDGE + x0, size)
-            first_rows = lax.rem(lanes((size, L)), SLOT) >= 4
-            centre = vslots[0, h, area_v, :]
-            away = [jnp.where(first_rows, halo[1, f, h, area, :], halo[2, f, h, area, :]) for f in range(2)]
-            away = [away[0], vslots[1, h, area_v, :], away[1]]
-            sums = [None] * 3
-            for d in range(1, 4):
-                for row, turn in ((ROW_AFTER, -d), (ROW_BEFORE, d)):
-                    near = [rolled(x, turn) for x in away]
-                    factor = rows[row + d - 1][0:1] * (centre + near[1])
-                    for f in range(3):
-                        term = factor * near[f]
-                        sums[f] = term if sums[f] is None else sums[f] + term
-            for f in range(3):
-                edges[h, f, area, :] = sums[f]
-
-    def normal_plane(z, carry):
-        turn = lax.rem(L - z, L)
-        turned = [[pltpu.roll(lines[n, pl.ds(8 * g, 8), :], turn, 1) for g in range(GROUPS)] for n in range(2)]
-        for tile in range(TILES):
-            group, at = tile // 4, 32 * (tile % 4)
-            below, total = (jnp.broadcast_to(turned[n][group][:, at:at + 1], (8, L)) for n in range(2))
-            area = pl.ds(8 * tile, 8)
-            vel[z, area, :] = frac * total - (crow[z, area, :] + below)
+    store_weights(weights, stencil)
+
+    source3 = lax.broadcasted_iota(jnp.int32, (2 * L, 2 * L), 0)
+    target3 = lanes((2 * L, 2 * L))
+    ones = (source3 // L == target3 // L).astype(F32).astype(BF16)
+    both = jnp.concatenate([parts[0], parts[1]], axis=1)
+    plane_of = lax.rem(lanes((WIDE, 2 * L)), 32)
+    group_planes = 4
+
+    def normal_planes(n, carry):
+        z0 = group_planes * n
+        chosen = [jnp.where(plane_of == z0 + k, both, 0.0).astype(BF16) for k in range(group_planes)]
+        found = jnp.dot(jnp.concatenate(chosen, axis=0), ones, preferred_element_type=F32)
+        for k in range(group_planes):
+            here = found[k * WIDE:k * WIDE + SPAN]
+            vel[z0 + k] = frac * here[:, L:] - (crow[z0 + k] + here[:, :L])
         return carry
 
-    lax.fori_loop(0, depth, normal_plane, 0, unroll=2)
+    lax.fori_loop(0, depth // group_planes, normal_planes, 0)
 
     def at(z, x0, d):
         return vel[z, pl.ds(EDGE + x0 + d, STEP), :]
@@ -436,8 +459,7 @@
         for x0 in range(0, L, STEP):
             v = at(z, x0, 0)
             for f, field in enumerate((q_at(0, z, x0, 0), v, q_at(1, z, x0, 0))):
-                left[pl.ds(f * L + x0, STEP), :] = pieces(field)
-                left[pl.ds((3 + f) * L + x0, STEP), :] = pieces(v * field)
+                left[pl.ds(f * L + x0, STEP), :] = pieces_of_two(field, v * field)
 
     def plane(z, left, right, later):
         turn = lax.rem(2 * L - 4 - SLOT * lax.rem(z, half), L)
@@ -457,8 +479,8 @@
                 others = result[z, 1, own, :] if f == 1 else part[f // 2, z, own, :]
                 turned = pltpu.roll(edges[z // half, f, own, :], turn, 1)
                 edge = jnp.where((lane < 4) | (lane >= L - 4), turned, 0.0)
-                slope, flux = right[pl.ds(f * L + x0, STEP), :], right[pl.ds((3 + f) * L + x0, STEP), :]
-                result[z, f, own, :] = others + (v * slope + flux) * scale + edge
+                both = right[pl.ds(f * L + x0, STEP), :]
+                result[z, f, own, :] = others + (v * both[:, :L] + both[:, L:]) * scale + edge
         pltpu.make_async_copy(result.at[z], out.at[:, z], out_sem.at[z]).start()
 
     split(0, left_even)
@@ -532,15 +554,14 @@
         scratch_shapes=[
             pltpu.VMEM((depth, SPAN, L), F32),
             pltpu.VMEM((depth, 3, L, L), F32),
-            pltpu.VMEM((3, halves, SPAN, L), F32),
+            pltpu.VMEM((3, WIDE, L), F32),
             pltpu.VMEM((2, halves, SPAN, L), F32),
             pltpu.VMEM((halves, 3, L, L), F32),
-            pltpu.VMEM((3 * L, L), BF16),
-            pltpu.VMEM((3 * L, L), BF16),
-            pltpu.VMEM((6 * L, 3 * L), BF16),
-            pltpu.VMEM((6 * L, 3 * L), BF16),
-            pltpu.VMEM((6 * L, L), F32),
-            pltpu.VMEM((6 * L, L), F32),
+            pltpu.VMEM((6 * L, 2 * L), BF16),
+            pltpu.VMEM((3 * L, 6 * L), BF16),
+            pltpu.VMEM((3 * L, 6 * L), BF16),
+            pltpu.VMEM((3 * L, 2 * L), F32),
+            pltpu.VMEM((3 * L, 2 * L), F32),
             dma((depth,)),
         ],
         compiler_params=pltpu.CompilerParams(vmem_limit_bytes=VMEM_SECOND),

time: 46.7 us -> 49.5 us (1.060)
  Pallas kernels: 46.6 us -> 49 us
    pallas_call x1, Pallas kernels: 27.4 us -> 33.4 us  [shards(): pl.pallas_call(functools.partial(first_kernel, n_gy, depth), out_shape=[p...]
    pallas_call x1, Pallas kernels: 19.2 us -> 15.6 us  [shards(): pl.pallas_call(functools.partial(second_kernel, depth), out_shape=jax.Sha...]
where the time goes in v2:
time: 49.5 us; the launch traced here: 49 us
  Pallas kernels  49 us (99%)
    pallas_call x1, Pallas kernels, shards(): pl.pallas_call(functools.partial(first_kernel, n_gy, depth), out_shape=[p...  33.4 us
    pallas_call x1, Pallas kernels, shards(): pl.pallas_call(functools.partial(second_kernel, depth), out_shape=jax.Sha...  15.6 us

profile of v2, /device:TPU:0, one launch (start us, length us, event | category | flops | bytes accessed | tf_op | source)
XLA Modules:
  0.0 49.0 jit_solution(6223340244859016516)
XLA Ops:
  0.0 33.4 %exchange.1 = (f32[2,32,144,128]{3,2,1,0:T(8,128)S(1)}, f32[32,136,128]{2,1,0:T(8,128)S(1)}, f32[3,2,2,128,128]{4,3,2,1,0:T(8,128)S(1)}, f32[3,2,136,128]{3,2,1,...) custom-call(f32[2,32,128,128]{3,2,1,0:T(8,128)} %vel.1, ...), custom_call_target="tpu_custom_call" | custom-call | tf_op jit(solution)/shard_map/exchange/pallas_call | solution.py:526
  33.4 15.6 %advect.1 = f32[3,32,128,128]{3,2,1,0:T(8,128)} custom-call(f32[2,32,144,128]{3,2,1,0:T(8,128)S(1)} %get-tuple-element.13.uw, f32[32,136,128]{2,1,0:T(8,128)S(1)} %get-tuple-element.14.crow, f32[3,2,2,128,128]{4,3,2,1,0:T(8,128)S(1)} %get-tuple-element.15.halo, f32[3,2,136,128]{3,2,1,0:T(8,128)S(1)} %get-tuple-element.16.shalo, ...), custom_call_target="tpu_custom_call" | custom-call | tf_op jit(solution)/shard_map/advect/pallas_call | solution.py:549

commit v3 on v2

--- a/solution.py
+++ b/solution.py
@@ -78,8 +78,8 @@
     return jnp.concatenate(three(x), axis=1)
 
 
-def pieces_of_two(x, y):
-    return jnp.concatenate([part for pair in zip(three(x), three(y)) for part in pair], axis=1)
+def pieces_of(*arrays):
+    return jnp.concatenate([part for same in zip(*map(three, arrays)) for part in same], axis=1)
 
 
 def skew(adv, fields):
@@ -108,11 +108,19 @@
     return total
 
 
+def store_weights(ref, matrix):
+    matrix = matrix.astype(BF16)
+    nothing = jnp.zeros((L, L), BF16)
+    for n in range(3):
+        ref[2 * n * L:(2 * n + 1) * L, :] = jnp.concatenate([matrix, nothing], axis=1)
+        ref[(2 * n + 1) * L:(2 * n + 2) * L, :] = jnp.concatenate([nothing, matrix], axis=1)
+
+
 def first_kernel(
     n_gy, depth,
     vel, sm_far, wm_far,
-    uw, crow, halo, shalo, part, lines, rows, m120,
-    slope, m_wide, ladder, stage_out, stage_in, sm, wm, left_even, left_odd,
+    uw, crow, halo, shalo, sland, part, lines, rows, m120,
+    slope, m_wide, ladder, narrowing, hpack, spack, stage_out, stage_in, sm, wm,
     load_sem, gx_send, gx_recv, y_send, y_recv, st_send, st_recv,
 ):
     gx, gy = lax.axis_index("gx"), lax.axis_index("gy")
@@ -203,11 +211,80 @@
     m_wide[HALO:HALO + L, :] = own_cols
     m_wide[HALO + L:WIDE, :] = other_cols[0:HALO, :]
     m120[...] = own_cols * (1.0 / 120.0)
-    source = lax.broadcasted_iota(jnp.int32, (L, 2 * L), 0)
-    target = lanes((L, 2 * L))
-    steps = jnp.where(source < target, 1.0, jnp.where(source == target, 0.5, 0.0)).astype(BF16)
+    source = lax.broadcasted_iota(jnp.int32, (L, L), 0)
+    target = lanes((L, L))
+    store_weights(ladder, jnp.where(source < target, 1.0, jnp.where(source == target, 0.5, 0.0)))
+
+    early = (gx == 0) | (gy < n_gy // 8)
+    ahead = jnp.where(gy == 0, (5 * depth) // 8, jnp.where((gx == 0) & (gy < n_gy // 2), depth // 4, 0))
+
+    def around(z, d):
+        return lax.rem(z + (depth + d), depth)
+
+    def plane_terms(z, starts):
+        for x0 in starts:
+            size = 16
+
+            def at(f):
+                return lambda d: uw[f, z, pl.ds(HALO + x0 + d, size), :]
+
+            def over(f):
+                return lambda d: uw[f, around(z, d), pl.ds(HALO + x0, size), :]
+
+            along_x = skew(at(0), (at(0), at(1)))
+            along_z = skew(over(1), (over(0), over(1)))
+            m = m120[pl.ds(x0, size), :]
+            for f in range(2):
+                part[f, z, pl.ds(x0, size), :] = m * along_x[f] + along_z[f] * (1.0 / 120.0)
+
+    def inner_terms(z, carry):
+        plane_terms(z, range(16, L - 16, 16))
+        return carry
+
+    def outer_terms(z, carry):
+        plane_terms(z, (0, L - 16))
+        return carry
+
+    def send_slots(source, landing, n):
+        copies = []
+        for side, where in enumerate((down_gy, up_gy)):
+            copies.append(pltpu.make_async_remote_copy(
+                src_ref=source.at[side], dst_ref=landing.at[side],
+                send_sem=y_send.at[n, side], recv_sem=y_recv.at[n, side],
+                device_id={"gy": where}, device_id_type=MESH))
+            copies[-1].start()
+        return copies
+
+    def pack(read, extent):
+        slot = lanes((extent, L)) // SLOT
+        result = []
+        for h in range(halves):
+            def body(z, packed):
+                return jnp.where(slot == z, pltpu.roll(read(h * half + z), SLOT * z + 4, 1), packed)
+
+            result.append(lax.fori_loop(0, half, body, jnp.zeros((extent, L), F32), unroll=4))
+        return result
+
+    def pack_fields():
+        for f in range(2):
+            both = jnp.dot(pieces_of(*pack(lambda z, f=f: uw[f, z, pl.ds(HALO, L), :], L)), narrowing[...],
+                           preferred_element_type=F32)
+            for side in range(2):
+                hpack[side, f] = both[:, side * L:(side + 1) * L]
+
+    from_row = lax.broadcasted_iota(jnp.int32, (halves * L, 2 * L), 0)
+    to_lane = lanes((halves * L, 2 * L))
+    lane, place8 = lax.rem(from_row, L), lax.rem(from_row, SLOT)
+    plane_lane = 4 * (half * (from_row // L) + lane // SLOT)
+    narrow = ((place8 >= 4) & (to_lane == plane_lane + place8 - 4)) | ((place8 < 4) & (to_lane == L + plane_lane + place8))
+    narrow = narrow.astype(F32).astype(BF16)
     for n in range(3):
-        ladder[n * L:(n + 1) * L, :] = steps
+        narrowing[n * halves * L:(n + 1) * halves * L, :] = narrow
+
+    for copy in loads:
+        copy.wait()
+    pl.when(early)(pack_fields)
+    lax.fori_loop(0, ahead, inner_terms, 0)
 
     pl.semaphore_wait(barrier, count)
 
@@ -220,65 +297,25 @@
                 device_id={"gx": other}, device_id_type=MESH))
             gx_copies[-1].start()
 
-    for copy in loads:
-        copy.wait()
-
-    def send_slots(array, n):
-        copies = []
-        for side, where in ((1, down_gy), (2, up_gy)):
-            copies.append(pltpu.make_async_remote_copy(
-                src_ref=array.at[0], dst_ref=array.at[side],
-                send_sem=y_send.at[n, side - 1], recv_sem=y_recv.at[n, side - 1],
-                device_id={"gy": where}, device_id_type=MESH))
-            copies[-1].start()
-        return copies
-
-    def pack(read, extent, store):
-        slot = lanes((extent, L)) // SLOT
-        for h in range(halves):
-            def body(z, packed):
-                return jnp.where(slot == z, pltpu.roll(read(h * half + z), SLOT * z + 4, 1), packed)
-
-            store(h, lax.fori_loop(0, half, body, jnp.zeros((extent, L), F32), unroll=4))
-
     for copy in gx_copies:
         copy.wait()
 
     lane_small = lanes((8, L))
     shift = HALO - EDGE
 
-    def around(z, d):
-        return lax.rem(z + (depth + d), depth)
-
-    def slope_split(z, left):
-        for x0, size in chunks(SPAN, 48):
+    def slope_plane(z, sums):
+        sums = list(sums)
+        for x0, size in chunks(SPAN, 8):
             du = slope_sum(lambda d: uw[0, z, pl.ds(shift + x0 + d, size), :])
             dw = slope_sum(lambda d: uw[1, around(z, d), pl.ds(shift + x0, size), :])
             value = (m_wide[pl.ds(shift + x0, size), :] * du + dw) * r60
             slope[z, pl.ds(x0, size), :] = value
-            left[pl.ds(min(x0, SPAN - size) + (SLOT if x0 + size == SPAN else 0), size), :] = pieces(value)
-
-    def row_in_left(row):
-        return row if row < SPAN - 48 else row + SLOT
-
-    def slope_climb(z, left, sums, later):
-        climbed = jnp.dot(left[...], ladder[...], preferred_element_type=F32)
-        slope_split(*later)
-        for tile in range(TILES):
-            row = row_in_left(8 * tile)
-            crow[z, pl.ds(8 * tile, 8), :] = climbed[row:row + 8, :L]
-            group, quarter = tile // 4, tile % 4
-            sums[group] = jnp.where(lane_small == 32 * quarter + z, climbed[row:row + 8, L:], sums[group])
-        return sums
-
-    slope_split(0, left_even)
-
-    def slope_plane(n, sums):
-        z = 2 * n
-        sums = slope_climb(z, left_even, list(sums), (z + 1, left_odd))
-        return tuple(slope_climb(z + 1, left_odd, sums, (around(z, 2), left_even)))
-
-    sums = lax.fori_loop(0, depth // 2, slope_plane, tuple(jnp.zeros((8, L), F32) for _ in range(GROUPS)))
+            group, quarter = x0 // 32, (x0 // 8) % 4
+            line = jnp.sum(value, axis=1, keepdims=True)
+            sums[group] = jnp.where(lane_small == 32 * quarter + z, line, sums[group])
+        return tuple(sums)
+
+    sums = lax.fori_loop(0, depth, slope_plane, tuple(jnp.zeros((8, L), F32) for _ in range(GROUPS)), unroll=2)
     own = jnp.concatenate(sums, axis=0)
     lines[2] = own
 
@@ -293,39 +330,36 @@
             copies[-1].start()
         return copies
 
-    def plane_terms(z, carry):
-        for x0, size in chunks(L, 16):
-            def at(f):
-                return lambda d: uw[f, z, pl.ds(HALO + x0 + d, size), :]
-
-            def over(f):
-                return lambda d: uw[f, around(z, d), pl.ds(HALO + x0, size), :]
-
-            along_x = skew(at(0), (at(0), at(1)))
-            along_z = skew(over(1), (over(0), over(1)))
-            m = m120[pl.ds(x0, size), :]
-            for f in range(2):
-                part[f, z, pl.ds(x0, size), :] = m * along_x[f] + along_z[f] * (1.0 / 120.0)
+    def climb(n, carry):
+        z = 2 * n
+        climbed = jnp.dot(pieces_of(slope[z], slope[z + 1]), ladder[...], preferred_element_type=F32)
+        crow[z] = climbed[:, :L]
+        crow[z + 1] = climbed[:, L:]
         return carry
 
+    y_copies = []
+
+    def work(stage):
+        if stage == 0:
+            pl.when(jnp.logical_not(early))(pack_fields)
+            y_copies.extend(send_slots(hpack, halo, 0))
+
+            for h, value in enumerate(pack(lambda z: slope[z], SPAN)):
+                shalo[h] = value
+            both = jnp.dot(pieces_of(*(shalo[h] for h in range(halves))), narrowing[...], preferred_element_type=F32)
+            for side in range(2):
+                spack[side] = both[:, side * L:(side + 1) * L]
+            y_copies.extend(send_slots(spack, sland, 1))
+        if stage == 1 % len(rings):
+            lax.fori_loop(0, depth // 2, climb, 0)
+        if stage == len(rings) - 1:
+            lax.fori_loop(0, depth, outer_terms, 0)
+
     below = jnp.zeros((PACKED, L), F32)
-    cut = [depth * k // len(rings) for k in range(len(rings) + 1)]
     for stage, (stride, size) in enumerate(rings):
         stage_out[stage] = own
         copies = send_stage(stage)
-        if stage == 0:
-            def store_slope(h, value):
-                shalo[0, h] = value
-
-            for f in range(2):
-                def store_halo(h, value, f=f):
-                    halo[0, f, h] = value
-
-                pack(lambda z, f=f: uw[f, z, pl.ds(HALO, L), :], L, store_halo)
-            y_copies = send_slots(halo, 0)
-            pack(lambda z: slope[z], SPAN, store_slope)
-            y_copies += send_slots(shalo, 1)
-        lax.fori_loop(cut[stage], cut[stage + 1], plane_terms, 0)
+        work(stage)
         mine = lax.rem(gy // stride, size)
         for copy in copies:
             copy.wait()
@@ -340,14 +374,15 @@
             below = lines[0]
     lines[0] = below
     lines[1] = own
+    lax.fori_loop(ahead, depth, inner_terms, 0)
 
     for copy in y_copies:
         copy.wait()
 
 
 def second_kernel(
-    depth, uw, crow, halo, shalo, part, lines, rows, m120,
-    out, vel, result, parts, vslots, edges, weights,
+    depth, uw, crow, halo, shalo, sland, part, lines, rows, m120,
+    out, vel, result, parts, vslots, edges, weights, widening, hwide,
     left_even, left_odd, right_even, right_odd, out_sem,
 ):
     half = min(HALF, depth)
@@ -360,13 +395,6 @@
 
     source = lax.broadcasted_iota(jnp.int32, (L, L), 0)
     target = lanes((L, L))
-
-    def store_weights(ref, matrix):
-        matrix = matrix.astype(BF16)
-        nothing = jnp.zeros((L, L), BF16)
-        for n in range(3):
-            ref[2 * n * L:(2 * n + 1) * L, :] = jnp.concatenate([matrix, nothing], axis=1)
-            ref[(2 * n + 1) * L:(2 * n + 2) * L, :] = jnp.concatenate([nothing, matrix], axis=1)
 
     packed = pieces(lines[...].reshape(3 * PACKED, L))
     from_lane = lax.broadcasted_iota(jnp.int32, (3 * L, L), 0)
@@ -394,12 +422,28 @@
     local = jnp.where(same_side & passed, 1.0, jnp.where(source == target, 0.5, 0.0)).astype(BF16)
     local = jnp.concatenate([local, local, local], axis=0)
     first_rows = lax.rem(lanes((SPAN, L)), SLOT) >= 4
+    from_row = lax.broadcasted_iota(jnp.int32, (2 * L, halves * L), 0)
+    to_lane = lanes((2 * L, halves * L))
+    place8 = lax.rem(to_lane, SLOT)
+    plane_lane = 4 * (half * (to_lane // L) + lax.rem(to_lane, L) // SLOT)
+    widen = ((place8 >= 4) & (from_row == plane_lane + place8 - 4)) | ((place8 < 4) & (from_row == L + plane_lane + place8))
+    widen = widen.astype(F32).astype(BF16)
+    for n in range(3):
+        widening[2 * n * L:2 * (n + 1) * L, :] = widen
+
+    def widened(first, last):
+        return jnp.dot(pieces_of(first, last), widening[...], preferred_element_type=F32)
+
+    for f in range(2):
+        wide = widened(halo[0, f], halo[1, f])
+        for h in range(halves):
+            hwide[h, f] = wide[:, h * L:(h + 1) * L]
+    swide = widened(sland[0], sland[1])
     spread = [jnp.dot(parts[n].astype(BF16), to_slot, preferred_element_type=F32) for n in range(3)]
     for h in range(halves):
         below, total, line = (x[:SPAN, h * L:(h + 1) * L] for x in spread)
-        near = jnp.dot(pieces(shalo[0, h]), local, preferred_element_type=F32)
-        away = jnp.where(first_rows, shalo[1, h], shalo[2, h])
-        away = jnp.dot(pieces(away), local, preferred_element_type=F32)
+        near = jnp.dot(pieces(shalo[h]), local, preferred_element_type=F32)
+        away = jnp.dot(pieces(swide[:, h * L:(h + 1) * L]), local, preferred_element_type=F32)
         near = jnp.where(first_rows, near, line - near)
         away = jnp.where(first_rows, line + away, -away)
         vslots[0, h] = rows[ROW_OWN][0:1] * total - (near + below)
@@ -414,11 +458,9 @@
     for h in range(halves):
         for x0, size in chunks(L, 32):
             area = pl.ds(x0, size)
-            first = lax.rem(lanes((size, L)), SLOT) >= 4
             v = vslots[1, h, pl.ds(EDGE + x0, size), :]
-            away = [jnp.where(first, halo[1, f, h, area, :], halo[2, f, h, area, :]) for f in range(2)]
-            for f, field in enumerate((away[0], v, away[1])):
-                left_even[pl.ds(f * L + x0, size), :] = pieces_of_two(field, v * field)
+            for f, field in enumerate((hwide[h, 0, area, :], v, hwide[h, 1, area, :])):
+                left_even[pl.ds(f * L + x0, size), :] = pieces_of(field, v * field)
         right_even[...] = jnp.dot(left_even[...], weights[...], preferred_element_type=F32)
         for x0, size in chunks(L, 32):
             v = vslots[0, h, pl.ds(EDGE + x0, size), :]
@@ -459,7 +501,7 @@
         for x0 in range(0, L, STEP):
             v = at(z, x0, 0)
             for f, field in enumerate((q_at(0, z, x0, 0), v, q_at(1, z, x0, 0))):
-                left[pl.ds(f * L + x0, STEP), :] = pieces_of_two(field, v * field)
+                left[pl.ds(f * L + x0, STEP), :] = pieces_of(field, v * field)
 
     def plane(z, left, right, later):
         turn = lax.rem(2 * L - 4 - SLOT * lax.rem(z, half), L)
@@ -513,8 +555,9 @@
     kept = [
         (2, depth, WIDE, L),
         (depth, SPAN, L),
-        (3, 2, halves, L, L),
-        (3, halves, SPAN, L),
+        (2, 2, L, L),
+        (halves, SPAN, L),
+        (2, SPAN, L),
         (2, depth, L, L),
         (3, PACKED, L),
         (ROWS, 8, L),
@@ -531,13 +574,14 @@
         scratch_shapes=[
             pltpu.VMEM((depth, SPAN, L), F32),
             pltpu.VMEM((WIDE, L), F32),
-            pltpu.VMEM((3 * L, 2 * L), BF16),
+            pltpu.VMEM((6 * L, 2 * L), BF16),
+            pltpu.VMEM((3 * halves * L, 2 * L), BF16),
+            pltpu.VMEM((2, 2, L, L), F32),
+            pltpu.VMEM((2, SPAN, L), F32),
             pltpu.VMEM((n_ring, PACKED, L), F32),
             pltpu.VMEM((n_ring, others, PACKED, L), F32),
             pltpu.VMEM((2, L), F32),
             pltpu.VMEM((n_gy, L), F32),
-            pltpu.VMEM((WIDE, 3 * L), BF16),
-            pltpu.VMEM((WIDE, 3 * L), BF16),
             dma((4,)), dma((2, 2)), dma((2, 2)), dma((2, 2)), dma((2, 2)),
             dma((n_ring, others)), dma((n_ring, others)),
         ],
@@ -558,6 +602,8 @@
             pltpu.VMEM((2, halves, SPAN, L), F32),
             pltpu.VMEM((halves, 3, L, L), F32),
             pltpu.VMEM((6 * L, 2 * L), BF16),
+            pltpu.VMEM((6 * L, halves * L), BF16),
+            pltpu.VMEM((halves, 2, L, L), F32),
             pltpu.VMEM((3 * L, 6 * L), BF16),
             pltpu.VMEM((3 * L, 6 * L), BF16),
             pltpu.VMEM((3 * L, 2 * L), F32),

time: 49.5 us -> 47.6 us (0.962)
  Pallas kernels: 49 us -> 46.8 us
    pallas_call x1, Pallas kernels: 33.4 us -> 31 us  [shards(): pl.pallas_call(functools.partial(first_kernel, n_gy, depth), out_shape=[p...]
where the time goes in v3:
time: 47.6 us; the launch traced here: 46.8 us
  Pallas kernels  46.8 us (98%)
    pallas_call x1, Pallas kernels, shards(): pl.pallas_call(functools.partial(first_kernel, n_gy, depth), out_shape=[p...  31 us
    pallas_call x1, Pallas kernels, shards(): pl.pallas_call(functools.partial(second_kernel, depth), out_shape=jax.Sha...  15.8 us

profile of v3, /device:TPU:0, one launch (start us, length us, event | category | flops | bytes accessed | tf_op | source)
XLA Modules:
  0.0 46.8 jit_solution(6763081210467386311)
XLA Ops:
  0.0 31.0 %exchange.1 = (f32[2,32,144,128]{3,2,1,0:T(8,128)S(1)}, f32[32,136,128]{2,1,0:T(8,128)S(1)}, f32[2,2,128,128]{3,2,1,0:T(8,128)S(1)}, f32[2,136,128]{2,1,0:T(8,12...) custom-call(f32[2,32,128,128]{3,2,1,0:T(8,128)} %vel.1, ...), custom_call_target="tpu_custom_call" | custom-call | tf_op jit(solution)/shard_map/exchange/pallas_call | solution.py:569
  31.0 15.8 %advect.1 = f32[3,32,128,128]{3,2,1,0:T(8,128)} custom-call(f32[2,32,144,128]{3,2,1,0:T(8,128)S(1)} %get-tuple-element.14.uw, f32[32,136,128]{2,1,0:T(8,128)S(1)} %get-tuple-element.15.crow, f32[2,2,128,128]{3,2,1,0:T(8,128)S(1)} %get-tuple-element.16.halo, f32[2,136,128]{2,1,0:T(8,128)S(1)} %get-tuple-element.17.shalo, ...), custom_call_target="tpu_custom_call" | custom-call | tf_op jit(solution)/shard_map/advect/pallas_call | solution.py:593

commit v4 on v3

--- a/solution.py
+++ b/solution.py
@@ -120,7 +120,7 @@
     n_gy, depth,
     vel, sm_far, wm_far,
     uw, crow, halo, shalo, sland, part, lines, rows, m120,
-    slope, m_wide, ladder, narrowing, hpack, spack, stage_out, stage_in, sm, wm,
+    slope, m_wide, ladder, narrowing, hpack, spack, stage_out, stage_in, sm, wm, left_even, left_odd,
     load_sem, gx_send, gx_recv, y_send, y_recv, st_send, st_recv,
 ):
     gx, gy = lax.axis_index("gx"), lax.axis_index("gy")
@@ -211,12 +211,12 @@
     m_wide[HALO:HALO + L, :] = own_cols
     m_wide[HALO + L:WIDE, :] = other_cols[0:HALO, :]
     m120[...] = own_cols * (1.0 / 120.0)
-    source = lax.broadcasted_iota(jnp.int32, (L, L), 0)
-    target = lanes((L, L))
-    store_weights(ladder, jnp.where(source < target, 1.0, jnp.where(source == target, 0.5, 0.0)))
-
-    early = (gx == 0) | (gy < n_gy // 8)
-    ahead = jnp.where(gy == 0, (5 * depth) // 8, jnp.where((gx == 0) & (gy < n_gy // 2), depth // 4, 0))
+    source = lax.broadcasted_iota(jnp.int32, (L, 2 * L), 0)
+    target = lanes((L, 2 * L))
+    steps = jnp.where(source < target, 1.0, jnp.where(source == target, 0.5, 0.0)).astype(BF16)
+    for n in range(3):
+        ladder[n * L:(n + 1) * L, :] = steps
+
 
     def around(z, d):
         return lax.rem(z + (depth + d), depth)
@@ -238,11 +238,7 @@
                 part[f, z, pl.ds(x0, size), :] = m * along_x[f] + along_z[f] * (1.0 / 120.0)
 
     def inner_terms(z, carry):
-        plane_terms(z, range(16, L - 16, 16))
-        return carry
-
-    def outer_terms(z, carry):
-        plane_terms(z, (0, L - 16))
+        plane_terms(z, range(0, L, 16))
         return carry
 
     def send_slots(source, landing, n):
@@ -283,8 +279,6 @@
 
     for copy in loads:
         copy.wait()
-    pl.when(early)(pack_fields)
-    lax.fori_loop(0, ahead, inner_terms, 0)
 
     pl.semaphore_wait(barrier, count)
 
@@ -297,25 +291,44 @@
                 device_id={"gx": other}, device_id_type=MESH))
             gx_copies[-1].start()
 
+    pack_fields()
+    y_copies = send_slots(hpack, halo, 0)
+
     for copy in gx_copies:
         copy.wait()
 
     lane_small = lanes((8, L))
     shift = HALO - EDGE
 
-    def slope_plane(z, sums):
-        sums = list(sums)
-        for x0, size in chunks(SPAN, 8):
+    def slope_split(z, left):
+        for x0, size in chunks(SPAN, 48):
             du = slope_sum(lambda d: uw[0, z, pl.ds(shift + x0 + d, size), :])
             dw = slope_sum(lambda d: uw[1, around(z, d), pl.ds(shift + x0, size), :])
             value = (m_wide[pl.ds(shift + x0, size), :] * du + dw) * r60
             slope[z, pl.ds(x0, size), :] = value
-            group, quarter = x0 // 32, (x0 // 8) % 4
-            line = jnp.sum(value, axis=1, keepdims=True)
-            sums[group] = jnp.where(lane_small == 32 * quarter + z, line, sums[group])
-        return tuple(sums)
-
-    sums = lax.fori_loop(0, depth, slope_plane, tuple(jnp.zeros((8, L), F32) for _ in range(GROUPS)), unroll=2)
+            left[pl.ds(min(x0, SPAN - size) + (SLOT if x0 + size == SPAN else 0), size), :] = pieces(value)
+
+    def row_in_left(row):
+        return row if row < SPAN - 48 else row + SLOT
+
+    def slope_climb(z, left, sums, later):
+        climbed = jnp.dot(left[...], ladder[...], preferred_element_type=F32)
+        slope_split(*later)
+        for tile in range(TILES):
+            row = row_in_left(8 * tile)
+            crow[z, pl.ds(8 * tile, 8), :] = climbed[row:row + 8, :L]
+            group, quarter = tile // 4, tile % 4
+            sums[group] = jnp.where(lane_small == 32 * quarter + z, climbed[row:row + 8, L:], sums[group])
+        return sums
+
+    slope_split(0, left_even)
+
+    def slope_plane(n, sums):
+        z = 2 * n
+        sums = slope_climb(z, left_even, list(sums), (z + 1, left_odd))
+        return tuple(slope_climb(z + 1, left_odd, sums, (around(z, 2), left_even)))
+
+    sums = lax.fori_loop(0, depth // 2, slope_plane, tuple(jnp.zeros((8, L), F32) for _ in range(GROUPS)))
     own = jnp.concatenate(sums, axis=0)
     lines[2] = own
 
@@ -330,30 +343,21 @@
             copies[-1].start()
         return copies
 
-    def climb(n, carry):
-        z = 2 * n
-        climbed = jnp.dot(pieces_of(slope[z], slope[z + 1]), ladder[...], preferred_element_type=F32)
-        crow[z] = climbed[:, :L]
-        crow[z + 1] = climbed[:, L:]
-        return carry
-
-    y_copies = []
+    first_cut, second_cut = ((depth * k) // 32 for k in (8, 20))
 
     def work(stage):
         if stage == 0:
-            pl.when(jnp.logical_not(early))(pack_fields)
-            y_copies.extend(send_slots(hpack, halo, 0))
-
             for h, value in enumerate(pack(lambda z: slope[z], SPAN)):
                 shalo[h] = value
             both = jnp.dot(pieces_of(*(shalo[h] for h in range(halves))), narrowing[...], preferred_element_type=F32)
             for side in range(2):
                 spack[side] = both[:, side * L:(side + 1) * L]
             y_copies.extend(send_slots(spack, sland, 1))
+            lax.fori_loop(0, first_cut, inner_terms, 0)
         if stage == 1 % len(rings):
-            lax.fori_loop(0, depth // 2, climb, 0)
+            lax.fori_loop(first_cut, second_cut, inner_terms, 0)
         if stage == len(rings) - 1:
-            lax.fori_loop(0, depth, outer_terms, 0)
+            lax.fori_loop(second_cut, depth, inner_terms, 0)
 
     below = jnp.zeros((PACKED, L), F32)
     for stage, (stride, size) in enumerate(rings):
@@ -374,8 +378,6 @@
             below = lines[0]
     lines[0] = below
     lines[1] = own
-    lax.fori_loop(ahead, depth, inner_terms, 0)
-
     for copy in y_copies:
         copy.wait()
 
@@ -574,7 +576,7 @@
         scratch_shapes=[
             pltpu.VMEM((depth, SPAN, L), F32),
             pltpu.VMEM((WIDE, L), F32),
-            pltpu.VMEM((6 * L, 2 * L), BF16),
+            pltpu.VMEM((3 * L, 2 * L), BF16),
             pltpu.VMEM((3 * halves * L, 2 * L), BF16),
             pltpu.VMEM((2, 2, L, L), F32),
             pltpu.VMEM((2, SPAN, L), F32),
@@ -582,6 +584,8 @@
             pltpu.VMEM((n_ring, others, PACKED, L), F32),
             pltpu.VMEM((2, L), F32),
             pltpu.VMEM((n_gy, L), F32),
+            pltpu.VMEM((WIDE, 3 * L), BF16),
+            pltpu.VMEM((WIDE, 3 * L), BF16),
             dma((4,)), dma((2, 2)), dma((2, 2)), dma((2, 2)), dma((2, 2)),
             dma((n_ring, others)), dma((n_ring, others)),
         ],

time: 47.6 us -> 42.6 us (0.89); the launches traced: 46.8 us -> 42.5 us
  Pallas kernels: 46.8 us -> 42.5 us
    pallas_call x1, Pallas kernels: 31 us -> 26.7 us  [shards(): pl.pallas_call(functools.partial(first_kernel, n_gy, depth), out_shape=[p...]
where the time goes in v4:
time: 42.6 us; the launch traced here: 42.5 us
  Pallas kernels  42.5 us (100%)
    pallas_call x1, Pallas kernels, shards(): pl.pallas_call(functools.partial(first_kernel, n_gy, depth), out_shape=[p...  26.7 us
    pallas_call x1, Pallas kernels, shards(): pl.pallas_call(functools.partial(second_kernel, depth), out_shape=jax.Sha...  15.8 us

profile of v4, /device:TPU:0, one launch (start us, length us, event | category | flops | bytes accessed | tf_op | source)
XLA Modules:
  0.0 42.5 jit_solution(9259681866204717791)
XLA Ops:
  0.0 26.7 %exchange.1 = (f32[2,32,144,128]{3,2,1,0:T(8,128)S(1)}, f32[32,136,128]{2,1,0:T(8,128)S(1)}, f32[2,2,128,128]{3,2,1,0:T(8,128)S(1)}, f32[2,136,128]{2,1,0:T(8,12...) custom-call(f32[2,32,128,128]{3,2,1,0:T(8,128)} %vel.1, ...), custom_call_target="tpu_custom_call" | custom-call | tf_op jit(solution)/shard_map/exchange/pallas_call | solution.py:571
  26.7 15.8 %advect.1 = f32[3,32,128,128]{3,2,1,0:T(8,128)} custom-call(f32[2,32,144,128]{3,2,1,0:T(8,128)S(1)} %get-tuple-element.14.uw, f32[32,136,128]{2,1,0:T(8,128)S(1)} %get-tuple-element.15.crow, f32[2,2,128,128]{3,2,1,0:T(8,128)S(1)} %get-tuple-element.16.halo, f32[2,136,128]{2,1,0:T(8,128)S(1)} %get-tuple-element.17.shalo, ...), custom_call_target="tpu_custom_call" | custom-call | tf_op jit(solution)/shard_map/advect/pallas_call | solution.py:597

commit v5 on v4

--- a/solution.py
+++ b/solution.py
@@ -258,7 +258,7 @@
             def body(z, packed):
                 return jnp.where(slot == z, pltpu.roll(read(h * half + z), SLOT * z + 4, 1), packed)
 
-            result.append(lax.fori_loop(0, half, body, jnp.zeros((extent, L), F32), unroll=4))
+            result.append(lax.fori_loop(0, half, body, jnp.zeros((extent, L), F32), unroll=half))
         return result
 
     def pack_fields():
@@ -491,7 +491,7 @@
             vel[z0 + k] = frac * here[:, L:] - (crow[z0 + k] + here[:, :L])
         return carry
 
-    lax.fori_loop(0, depth // group_planes, normal_planes, 0)
+    lax.fori_loop(0, depth // group_planes, normal_planes, 0, unroll=2)
 
     def at(z, x0, d):
         return vel[z, pl.ds(EDGE + x0 + d, STEP), :]

time: 42.6 us -> 41.1 us (0.965)
  Pallas kernels: 42.5 us -> 41 us
    pallas_call x1, Pallas kernels: 26.7 us -> 25.9 us  [shards(): pl.pallas_call(functools.partial(first_kernel, n_gy, depth), out_shape=[p...]
    pallas_call x1, Pallas kernels: 15.8 us -> 15.1 us  [shards(): pl.pallas_call(functools.partial(second_kernel, depth), out_shape=jax.Sha...]
where the time goes in v5:
time: 41.1 us; the launch traced here: 41 us
  Pallas kernels  41 us (100%)
    pallas_call x1, Pallas kernels, shards(): pl.pallas_call(functools.partial(first_kernel, n_gy, depth), out_shape=[p...  25.9 us
    pallas_call x1, Pallas kernels, shards(): pl.pallas_call(functools.partial(second_kernel, depth), out_shape=jax.Sha...  15.1 us

profile of v5, /device:TPU:0, one launch (start us, length us, event | category | flops | bytes accessed | tf_op | source)
XLA Modules:
  0.0 41.0 jit_solution(4116435955869781920)
XLA Ops:
  0.0 25.9 %exchange.1 = (f32[2,32,144,128]{3,2,1,0:T(8,128)S(1)}, f32[32,136,128]{2,1,0:T(8,128)S(1)}, f32[2,2,128,128]{3,2,1,0:T(8,128)S(1)}, f32[2,136,128]{2,1,0:T(8,12...) custom-call(f32[2,32,128,128]{3,2,1,0:T(8,128)} %vel.1, ...), custom_call_target="tpu_custom_call" | custom-call | tf_op jit(solution)/shard_map/exchange/pallas_call | solution.py:571
  25.9 15.1 %advect.1 = f32[3,32,128,128]{3,2,1,0:T(8,128)} custom-call(f32[2,32,144,128]{3,2,1,0:T(8,128)S(1)} %get-tuple-element.14.uw, f32[32,136,128]{2,1,0:T(8,128)S(1)} %get-tuple-element.15.crow, f32[2,2,128,128]{3,2,1,0:T(8,128)S(1)} %get-tuple-element.16.halo, f32[2,136,128]{2,1,0:T(8,128)S(1)} %get-tuple-element.17.shalo, ...), custom_call_target="tpu_custom_call" | custom-call | tf_op jit(solution)/shard_map/advect/pallas_call | solution.py:597

commit v6 on v5

--- a/solution.py
+++ b/solution.py
@@ -328,7 +328,7 @@
         sums = slope_climb(z, left_even, list(sums), (z + 1, left_odd))
         return tuple(slope_climb(z + 1, left_odd, sums, (around(z, 2), left_even)))
 
-    sums = lax.fori_loop(0, depth // 2, slope_plane, tuple(jnp.zeros((8, L), F32) for _ in range(GROUPS)))
+    sums = lax.fori_loop(0, depth // 2, slope_plane, tuple(jnp.zeros((8, L), F32) for _ in range(GROUPS)), unroll=2)
     own = jnp.concatenate(sums, axis=0)
     lines[2] = own
 

time: 41.1 us -> 40 us (0.973)
  Pallas kernels: 41 us -> 39.9 us
    pallas_call x1, Pallas kernels: 25.9 us -> 24.8 us  [shards(): pl.pallas_call(functools.partial(first_kernel, n_gy, depth), out_shape=[p...]
where the time goes in v6:
time: 40 us; the launch traced here: 39.9 us
  Pallas kernels  39.9 us (100%)
    pallas_call x1, Pallas kernels, shards(): pl.pallas_call(functools.partial(first_kernel, n_gy, depth), out_shape=[p...  24.8 us
    pallas_call x1, Pallas kernels, shards(): pl.pallas_call(functools.partial(second_kernel, depth), out_shape=jax.Sha...  15.1 us

profile of v6, /device:TPU:0, one launch (start us, length us, event | category | flops | bytes accessed | tf_op | source)
XLA Modules:
  0.0 39.9 jit_solution(9336118122785500221)
XLA Ops:
  0.0 24.8 %exchange.1 = (f32[2,32,144,128]{3,2,1,0:T(8,128)S(1)}, f32[32,136,128]{2,1,0:T(8,128)S(1)}, f32[2,2,128,128]{3,2,1,0:T(8,128)S(1)}, f32[2,136,128]{2,1,0:T(8,12...) custom-call(f32[2,32,128,128]{3,2,1,0:T(8,128)} %vel.1, ...), custom_call_target="tpu_custom_call" | custom-call | tf_op jit(solution)/shard_map/exchange/pallas_call | solution.py:571
  24.8 15.1 %advect.1 = f32[3,32,128,128]{3,2,1,0:T(8,128)} custom-call(f32[2,32,144,128]{3,2,1,0:T(8,128)S(1)} %get-tuple-element.14.uw, f32[32,136,128]{2,1,0:T(8,128)S(1)} %get-tuple-element.15.crow, f32[2,2,128,128]{3,2,1,0:T(8,128)S(1)} %get-tuple-element.16.halo, f32[2,136,128]{2,1,0:T(8,128)S(1)} %get-tuple-element.17.shalo, ...), custom_call_target="tpu_custom_call" | custom-call | tf_op jit(solution)/shard_map/advect/pallas_call | solution.py:597
